TPU v7x, 256 devices: a whole 4x4x8 slice. The times are simulated.
256 devices in a mesh: row: 8 (over x, z_hi), col: 32 (over z_lo, y, core).
Axes of the slice: x: 4, y: 4, z: 8 (z_hi: 2, z_lo: 4; z = z_hi * 4 + z_lo), core: 2. Of those that a mesh axis runs over, the one named last changes fastest.
Arguments:
- pair: float32 [1024, 1024, 128], P('row', 'col'), may hold values from -6 to 6
- single: float32 [1024, 384], P(('row', 'col')), may hold values from -6 to 6
- target_bins: int32 [1024, 1024], P('row', 'col'), may hold values from 0 to 63
- token_pad: int32 [1024], P(('row', 'col')), may hold values from 0 to 1, as said below
- w_gate: float32 [128, 512], replicated, may hold values from -0.5 to 0.5
- w_up: float32 [128, 512], replicated, may hold values from -0.5 to 0.5
- w_out: float32 [512, 128], replicated, may hold values from -0.25 to 0.25
- w_bias: float32 [128, 16], replicated, may hold values from -25 to 25
- w_query: float32 [384, 384], replicated, may hold values from -0.3125 to 0.3125
- w_key: float32 [384, 384], replicated, may hold values from -0.3125 to 0.3125
- w_value: float32 [384, 384], replicated, may hold values from -0.3125 to 0.3125
- w_gating: float32 [384, 384], replicated, may hold values from -0.3125 to 0.3125
- w_attn_out: float32 [384, 384], replicated, may hold values from -0.3125 to 0.3125
- w_dist: float32 [128, 64], replicated, may hold values from -12 to 12
- b_dist: float32 [64], replicated, may hold values from -2 to 2
Outputs:
- pair_out: float32 [1024, 1024, 128], P('row', 'col')
- single_out: float32 [1024, 384], P(('row', 'col'))
Inputs may be any that keep to these rules, and one draw needn't show every extreme that they name: `token_pad`: 1 for the first tokens and 0 for the rest, with at least 512 ones.
All inputs are finite; a program needn't handle non-finite values.
Results may differ from a plain program's by a relative error of at most 0.0003.
Values sent between devices are 32-bit elements; how exact they have to be, the bound alone decides.
No kernel may reach another device: no remote copies, remote signals or barrier semaphores. Data moves between devices by JAX's collectives and lax.ppermute only.
A program may use at most 64 MiB of HBM per device.

v0:
```python
import jax
import jax.numpy as jnp
from jax import lax
from jax.experimental import pallas as pl
from jax.experimental.pallas import tpu as pltpu
from jax.sharding import Mesh, PartitionSpec as P


F32 = jnp.float32
BF16 = jnp.bfloat16
ALL = ("x", "zh", "zl", "yh", "yl", "core")
COL = ("zl", "yh", "yl", "core")
PLANE = ("x", "yh", "yl", "core")
SIZES = (4, 2, 4, 2, 2, 2)


def flat_index(coords):
    index = 0
    for c, n in zip(coords, SIZES):
        index = index * n + c
    return index


def all_coords():
    out = [()]
    for n in SIZES:
        out = [c + (k,) for c in out for k in range(n)]
    return out


def halves(x):
    hi = x.astype(BF16)
    lo = (x - hi.astype(F32)).astype(BF16)
    return hi, lo


def mm(a, b):
    return jnp.dot(a, b, preferred_element_type=F32)


def mm_nt(a, b):
    return lax.dot_general(a, b, (((1,), (1,)), ((), ())), preferred_element_type=F32)


def mm3(a, b, dot=mm):
    ah, al = halves(a)
    bh, bl = halves(b)
    return dot(ah, bh) + (dot(al, bh) + dot(ah, bl))


def norm(x):
    mean = jnp.mean(x, axis=-1, keepdims=True)
    centred = x - mean
    var = jnp.mean(centred * centred, axis=-1, keepdims=True)
    return centred * lax.rsqrt(var + 1e-05)


def lanes_of(shape):
    return lax.broadcasted_iota(jnp.int32, shape, len(shape) - 1)


def doubled_projection(wdt_ref):
    d = wdt_ref[...]
    d = d - d[0:1, :]
    z = jnp.zeros_like(d)
    both = jnp.concatenate(
        [jnp.concatenate([d, z], axis=1), jnp.concatenate([z, d], axis=1)], axis=0
    )
    hi, lo = halves(both.T)
    return jnp.concatenate([hi, lo], axis=1)


def project(a, b, wp_ref):
    xh, xl = halves(jnp.concatenate([a, b], axis=1))
    p = mm(xh, wp_ref[...])
    return p[:, :128] + (p[:, 128:] + mm(xl, wp_ref[:, :128]))


def transition_kernel(
    pair_ref, tt_ref, wg_ref, wu_ref, wo_ref, wdt_ref, mid_ref, proj_ref, w1_ref, w2_ref, wp_ref
):
    step = pl.program_id(0)

    @pl.when(step == 0)
    def _():
        for k, ref in enumerate((wg_ref, wu_ref)):
            hi, lo = halves(ref[...])
            w1_ref[k, 0] = jnp.concatenate([hi, hi], axis=0)
            w1_ref[k, 1] = jnp.concatenate([lo, lo], axis=0)
        hi, lo = halves(wo_ref[...])
        w2_ref[...] = jnp.concatenate([hi, lo], axis=1)
        wp_ref[...] = doubled_projection(wdt_ref)

    x = pair_ref[...].reshape(1024, 128)
    nh, nl = halves(norm(x))
    both = jnp.concatenate([nh, nl], axis=1)
    out = jnp.zeros((1024, 128), F32)
    for c in range(0, 512, 256):
        gate = mm(both, w1_ref[0, 0, :, c : c + 256]) + mm(both, w1_ref[0, 1, :, c : c + 256])
        up = mm(both, w1_ref[1, 0, :, c : c + 256]) + mm(both, w1_ref[1, 1, :, c : c + 256])
        hidden = gate / (1.0 + jnp.exp(-gate)) * up
        hh, hl = halves(hidden)
        o = mm(hh, w2_ref[c : c + 256, :])
        out = out + (o[:, :128] + (o[:, 128:] + mm(hl, w2_ref[c : c + 256, :128])))
    mid = x + out
    mid_ref[...] = mid.reshape(4, 2, 4, 32, 128)
    split = mid.reshape(32, 2, 16, 128)
    proj = project(split[:, 0].reshape(512, 128), split[:, 1].reshape(512, 128), wp_ref)
    turned = pltpu.roll(tt_ref[...].astype(F32), (128 - 8 * step) % 128, 1)
    lane = lanes_of((16, 128))
    for k in range(4):
        for st in range(2):
            for w in range(4):
                i = k * 32 + st * 4 + w
                a = turned[0:16, i : i + 1]
                b = turned[16:32, i : i + 1]
                mark = jnp.where(lane == 0, a, jnp.where(lane == 64, b, 0.0))
                n = (k * 8 + st * 4 + w) * 16
                proj_ref[st, k, w] = proj[n : n + 16] + mark


def bias_kernel(mid_ref, wb_ref, bias_ref, w3_ref, n_ref):
    @pl.when(pl.program_id(0) == 0)
    def _():
        w = jnp.concatenate([wb_ref[...]] * 8, axis=1)
        lane = lanes_of((128, 128))
        for k in range(8):
            hi, lo = halves(jnp.where(lane // 16 == k, w, 0.0))
            row = jnp.concatenate([hi, lo], axis=1)
            w3_ref[k] = jnp.concatenate([row, row], axis=0)

    n_ref[...] = norm(mid_ref[...])
    acc = jnp.zeros((256, 256), F32)
    for k in range(8):
        x = jnp.concatenate(
            [n_ref[pl.ds(g * 8 + k, 64, stride=32), :] for g in range(4)], axis=0
        )
        hi, lo = halves(x)
        acc = acc + mm(jnp.concatenate([hi, lo], axis=1), w3_ref[k])
    acc = acc[:, :128] + acc[:, 128:]
    for g in range(4):
        bias_ref[:, g * 128 : (g + 1) * 128] = acc[g * 64 : (g + 1) * 64]


def pick_matrix():
    row = lax.broadcasted_iota(jnp.int32, (128, 128), 0)
    return jnp.where((row // 64 == lanes_of((128, 128)) // 64) & (row % 64 == 0), 1.0, 0.0).astype(BF16)


def own_kernel(proj_ref, bd_ref, own_ref, hits_ref):
    front = proj_ref[0:4, 0].reshape(256, 128)
    back = proj_ref[4:8, 0].reshape(256, 128)
    left = lanes_of((256, 128)) < 64
    own_a = jnp.where(left, front, pltpu.roll(back, 64, 1)).reshape(16, 16, 128)
    own_b = jnp.where(left, pltpu.roll(front, 64, 1), back).reshape(16, 16, 128)
    own = jnp.concatenate([own_a, own_b], axis=1).reshape(512, 128)
    bins = lanes_of((512, 128)) % 64
    mark = jnp.where(bins == 0, own, 0.0)
    target = mm(mark.astype(BF16), pick_matrix())
    bd = bd_ref[...]
    bd = bd - bd[:, 0:1]
    own_ref[...] = (own - mark + jnp.concatenate([bd, bd], axis=1)).reshape(16, 32, 128)
    hits = jnp.where(bins.astype(F32) == target, 1.0, 0.0).astype(BF16)
    hits_ref[...] = hits.reshape(16, 32, 128)


def attention_kernel(
    xr_ref, xc_ref, bias_ref, wq_ref, wk_ref, wv_ref, msg_ref, rowpad_ref, colpad_ref
):
    def tokens(ref, n):
        x = jnp.concatenate([ref[pl.ds(q, n, stride=4), :] for q in range(3)], axis=1)
        return norm(x), ref[pl.ds(3, n, stride=4), :][:, 0:1]

    rows, row_pad = tokens(xr_ref, 128)
    cols, col_pad = tokens(xc_ref, 32)
    lane = lanes_of((16, 128))
    for m in range(4):
        a = row_pad[m * 32 : m * 32 + 16]
        b = row_pad[m * 32 + 16 : m * 32 + 32]
        rowpad_ref[m * 16 : (m + 1) * 16, :] = jnp.where(lane < 64, a, b)
    colpad_ref[...] = jnp.broadcast_to(col_pad, (32, 128))
    query = mm3(rows, wq_ref[...]) * (24.0**-0.5)
    key = mm3(cols, wk_ref[...])
    value = mm3(cols, wv_ref[...])
    of_head = lanes_of((16, 384)) // 24 == lax.broadcasted_iota(jnp.int32, (16, 384), 0)

    def spread(y):
        return jnp.where(of_head[None], y[:, None, :], 0.0).reshape(512, 384)

    scores = mm3(query, spread(key), mm_nt) + bias_ref[...]
    of_key = lanes_of((32, 512)) // 16 == lax.broadcasted_iota(jnp.int32, (32, 512), 0)
    pad_lane = jnp.sum(jnp.where(of_key, col_pad, 0.0), axis=0, keepdims=True)
    scores = jnp.where(pad_lane > 0.5, scores, -1000000000.0)

    def over_keys(y, op):
        r = op(op(y[:, :128], y[:, 128:256]), op(y[:, 256:384], y[:, 384:]))
        for shift in (16, 32, 64):
            r = op(r, pltpu.roll(r, shift, 1))
        return r

    top = over_keys(scores, jnp.maximum)
    expo = jnp.exp(scores - jnp.concatenate([top] * 4, axis=1))
    total = over_keys(expo, jnp.add)
    acc = mm3(expo, spread(value))
    lane = lanes_of((128, 128))
    tail = jnp.where(lane < 16, total, jnp.where(lane < 32, top, 0.0))
    for q in range(3):
        msg_ref[pl.ds(q, 128, stride=4), :] = acc[:, q * 128 : (q + 1) * 128]
    msg_ref[pl.ds(3, 128, stride=4), :] = tail


def merge_kernel(msg_ref, single_ref, wg_ref, wo_ref, out_ref):
    lane = lanes_of((32, 128))
    accs, factors, totals = [], [], []
    for t in range(4):
        part = [msg_ref[pl.ds(4 * t + q, 32, stride=16), :] for q in range(4)]
        accs.append(jnp.concatenate(part[:3], axis=1))
        tail = part[3]
        local = pltpu.roll(tail, 112, 1)
        top = jnp.max(local, axis=0, keepdims=True)
        f = jnp.where(lane < 16, jnp.exp(local - top), 0.0)
        factors.append(f)
        totals.append(jnp.sum(f * tail, axis=0, keepdims=True))
    expand = jnp.where(
        lanes_of((128, 384)) // 24 == lax.broadcasted_iota(jnp.int32, (128, 384), 0), 1.0, 0.0
    )
    stacked = jnp.concatenate(factors + totals + totals, axis=0)
    wide = jnp.dot(stacked, expand, precision=lax.Precision.HIGHEST, preferred_element_type=F32)
    rows = []
    for t in range(4):
        num = jnp.sum(wide[t * 32 : (t + 1) * 32] * accs[t], axis=0, keepdims=True)
        rows.append(num / wide[128 + t : 129 + t])
    attended = jnp.concatenate(rows, axis=0)
    single = single_ref[...]
    g = mm3(norm(single), wg_ref[...])
    out_ref[...] = single + mm3(attended / (1.0 + jnp.exp(-g)), wo_ref[...])


def gradient_kernel(place_ref, *refs):
    parts = refs[:8]
    own_ref, hits_ref, mid_ref, rowpad_ref, colpad_ref, wdt_ref, out_ref = refs[8:15]
    f_ref, w_ref, ones_ref, pick_ref, d_ref = refs[15:]

    @pl.when(pl.program_id(0) == 0)
    def _():
        d = wdt_ref[...]
        z = jnp.zeros_like(d)
        both = jnp.concatenate(
            [jnp.concatenate([d, z], axis=1), jnp.concatenate([z, d], axis=1)], axis=0
        )
        hi, lo = halves(both)
        w_ref[0] = jnp.concatenate([hi, hi], axis=0)
        w_ref[1] = jnp.concatenate([lo, lo], axis=0)
        row = lax.broadcasted_iota(jnp.int32, (256, 128), 0) % 128
        same = row // 64 == lanes_of((256, 128)) // 64
        ones_ref[...] = jnp.where(same, 1.0, 0.0).astype(BF16)
        pick_ref[...] = pick_matrix()

    for p in range(8):
        place = place_ref[0] ^ p
        f_ref[pl.ds(pl.multiple_of(place * 64, 64), 64), :] = parts[p][0]

    lane = lanes_of((512, 128))
    first = lane < 64
    bins = lane % 64
    flip = jnp.concatenate([f_ref[pl.ds(i, 32, stride=16), :] for i in range(16)], axis=0)
    mark = jnp.where(bins == 0, flip, 0.0)
    target = mm(mark.astype(BF16), pick_ref[...])
    logits = own_ref[...].reshape(512, 128) + (flip - mark)
    top_a = jnp.max(jnp.where(first, logits, -3.0e38), axis=-1, keepdims=True)
    top_b = jnp.max(jnp.where(first, -3.0e38, logits), axis=-1, keepdims=True)
    expo = jnp.exp(logits - jnp.where(first, top_a, top_b))
    hi, lo = halves(expo)
    total = mm(jnp.concatenate([hi, lo], axis=1), ones_ref[...])
    hits = jnp.where(bins.astype(F32) == target, 1.0, 0.0) + hits_ref[...].reshape(512, 128).astype(F32)
    mask = rowpad_ref[...][:, None, :] * colpad_ref[...][None]
    hi, lo = halves(mask.reshape(512, 128) * (expo * (2.0 / total) - hits))
    d_ref[...] = jnp.concatenate([hi, lo], axis=1)
    change = mm(d_ref[...], w_ref[0]) + mm(d_ref[...], w_ref[1])
    for k in range(2):
        out_ref[0, k] = mid_ref[0, k] + change[:, k * 128 : (k + 1) * 128].reshape(16, 32, 128)


def tokens_kernel(single_ref, pad_ref, out_ref):
    tile = []
    for t in range(4):
        for q in range(3):
            tile.append(single_ref[t : t + 1, q * 128 : (q + 1) * 128])
        tile.append(jnp.full((1, 128), pad_ref[t].astype(F32)))
    out_ref[...] = jnp.broadcast_to(jnp.concatenate(tile, axis=0)[None], (32, 16, 128))


def full(shape):
    return pl.BlockSpec(shape, lambda *_: (0,) * len(shape))


def struct(*shape):
    return jax.ShapeDtypeStruct(shape, F32)


def per_device(
    pair,
    single,
    target_bins,
    token_pad,
    w_gate,
    w_up,
    w_out,
    w_bias,
    w_query,
    w_key,
    w_value,
    w_gating,
    w_attn_out,
    w_dist,
    b_dist,
):
    at = {name: lax.axis_index(name) for name in ALL}
    coords = all_coords()
    tt = target_bins.T
    wdt = w_dist.T

    tok = pl.pallas_call(
        tokens_kernel,
        in_specs=[full((4, 384)), pl.BlockSpec(memory_space=pltpu.SMEM)],
        out_shape=struct(32, 16, 128),
        name="tokens",
    )(single, token_pad)
    rows_tok = lax.all_to_all(tok, COL, split_axis=0, concat_axis=0, tiled=True)
    rows_tok = rows_tok.reshape(512, 128)

    mid, proj = pl.pallas_call(
        transition_kernel,
        grid=(4,),
        in_specs=[
            pl.BlockSpec((4, 2, 4, 32, 128), lambda s: (0, s, 0, 0, 0)),
            full((32, 128)),
            full((128, 512)),
            full((128, 512)),
            full((512, 128)),
            full((64, 128)),
        ],
        out_specs=[
            pl.BlockSpec((4, 2, 4, 32, 128), lambda s: (0, s, 0, 0, 0)),
            pl.BlockSpec((2, 4, 4, 16, 128), lambda s: (s, 0, 0, 0, 0)),
        ],
        out_shape=[struct(4, 8, 4, 32, 128), struct(8, 4, 4, 16, 128)],
        scratch_shapes=[
            pltpu.VMEM((2, 2, 256, 512), BF16),
            pltpu.VMEM((512, 256), BF16),
            pltpu.VMEM((256, 256), BF16),
        ],
        name="transition",
    )(pair.reshape(4, 8, 4, 32, 128), tt, w_gate, w_up, w_out, wdt)

    spread = lax.all_to_all(
        proj.reshape(32, 64, 128), PLANE, split_axis=0, concat_axis=0, tiled=True
    ).reshape(8, 4, 64, 128)

    quarter = lax.dynamic_slice_in_dim(rows_tok, (at["yl"] * 2 + at["core"]) * 128, 128, 0)
    perm = [(flat_index(c), flat_index((c[2], c[3], c[0], c[1], c[4], c[5]))) for c in coords]
    cols_tok = lax.ppermute(quarter, ALL, perm)

    bias = pl.pallas_call(
        bias_kernel,
        grid=(2,),
        in_specs=[pl.BlockSpec((2048, 128), lambda m: (m, 0)), full((128, 16))],
        out_specs=pl.BlockSpec((64, 512), lambda m: (m, 0)),
        out_shape=struct(128, 512),
        scratch_shapes=[pltpu.VMEM((8, 256, 256), BF16), pltpu.VMEM((2048, 128), F32)],
        name="bias",
    )(mid.reshape(4096, 128), w_bias)

    own, hits = pl.pallas_call(
        own_kernel,
        grid=(4,),
        in_specs=[pl.BlockSpec((8, 1, 4, 16, 128), lambda m: (0, m, 0, 0, 0)), full((1, 64))],
        out_specs=[pl.BlockSpec((16, 32, 128), lambda m: (m, 0, 0))] * 2,
        out_shape=[struct(64, 32, 128), jax.ShapeDtypeStruct((64, 32, 128), BF16)],
        name="own",
    )(proj, b_dist[None])

    msg, rowpad, colpad = pl.pallas_call(
        attention_kernel,
        out_shape=[struct(512, 128), struct(64, 128), struct(32, 128)],
        name="attention",
    )(rows_tok, cols_tok, bias, w_query, w_key, w_value)

    parts = []
    for n in range(8):
        u, v = n // 2, n % 2
        piece = lax.dynamic_index_in_dim(
            spread, (at["x"] ^ u) * 2 + (at["yh"] ^ v), 0, keepdims=False
        )
        perm = []
        for c in coords:
            x, zh, zl, yh, yl, core = c
            perm.append((flat_index(c), flat_index((zl, yh ^ v, x ^ u, zh, yl, core))))
        parts.append(lax.ppermute(piece, ALL, perm))
    place = (at["zl"] * 2 + at["zh"]).reshape(1)

    merged = lax.all_to_all(msg.reshape(32, 16, 128), COL, split_axis=0, concat_axis=0, tiled=True)
    merged = merged.reshape(512, 128)
    single_out = pl.pallas_call(
        merge_kernel, out_shape=struct(4, 384), name="merge"
    )(merged, single, w_gating, w_attn_out)

    grouped = pl.BlockSpec((1, 2, 16, 32, 128), lambda m, _: (m, 0, 0, 0, 0))
    pair_out = pl.pallas_call(
        gradient_kernel,
        grid_spec=pltpu.PrefetchScalarGridSpec(
            num_scalar_prefetch=1,
            grid=(4,),
            in_specs=[pl.BlockSpec((1, 64, 128), lambda m, _: (m, 0, 0))] * 8
            + [
                pl.BlockSpec((16, 32, 128), lambda m, _: (m, 0, 0)),
                pl.BlockSpec((16, 32, 128), lambda m, _: (m, 0, 0)),
                grouped,
                pl.BlockSpec((16, 128), lambda m, _: (m, 0)),
                full((32, 128)),
                full((64, 128)),
            ],
            out_specs=grouped,
            scratch_shapes=[
                pltpu.VMEM((512, 128), F32),
                pltpu.VMEM((2, 256, 256), BF16),
                pltpu.VMEM((256, 128), BF16),
                pltpu.VMEM((128, 128), BF16),
                pltpu.VMEM((512, 256), BF16),
            ],
        ),
        out_shape=struct(4, 2, 16, 32, 128),
        name="gradient",
    )(
        place,
        *parts,
        own,
        hits,
        mid.reshape(4, 2, 16, 32, 128),
        rowpad,
        colpad,
        wdt,
    )
    pair_out = pair_out.reshape(128, 32, 128)
    return (pair_out, single_out)


def solution(mesh):
    fine = Mesh(mesh.devices.reshape(SIZES), ALL)
    row, col = ("x", "zh"), COL
    in_specs = (
        P(row, col, None),
        P(ALL, None),
        P(row, col),
        P(ALL),
    ) + (P(),) * 11
    out_specs = (P(row, col, None), P(ALL, None))
    return jax.shard_map(
        per_device, mesh=fine, in_specs=in_specs, out_specs=out_specs, check_vma=False
    )
```

profile of v0, /device:TPU:32, one launch (start us, length us, event | category | flops | bytes accessed | tf_op | source)
XLA Modules:
  0.0 113.7 jit_solution(17243281232130543125)
XLA Ops:
  0.6 1.5 %tokens.1 = f32[32,16,128]{2,1,0:T(8,128)} custom-call(f32[4,384]{1,0:T(4,128)} %single_ref.3, s32[4]{0:T(128)} %pad_ref.1), custom_call_target="tpu_custom_call" | custom-call | tf_op jit(solution)/shard_map/tokens/pallas_call | solution.py:323
  2.2 8.8 %all-to-all-start.1 = ((f32[32,16,128]{2,1,0:T(8,128)}), f32[32,16,128]{2,1,0:T(8,128)S(1)}, u32[]{:S(2)}, u32[]{:S(2)}) async-start(f32[32,16,128]{2,1,0:T(8,128)} %tokens.1), calls=%async_computation.1 | async-start | bytes 524288 | tf_op jit(solution)/shard_map/all_to_all | solution.py:329
  11.0 0.0 copy-start.11
  11.0 12.3 %transition.1 = (f32[4,8,4,32,128]{4,3,2,1,0:T(8,128)}, f32[8,4,4,16,128]{4,3,2,1,0:T(8,128)}) custom-call(f32[4,8,4,32,128]{4,3,2,1,0:T(8,128)} %bitcast.33, s32[32,128]{1,0:T(8,128)} %bitcast.41, f32[128,512]{1,0:T(8,128)} %wg_ref.2, f32[128,512]{1,0:T(8,128)} %wu_ref.1, f32[512,128]{1,0:T(8,128)} %wo_ref.2, f32[64,128]{1,0:T(8,128)} %bitcast.39), custom_call_target="tpu_custom_call" | custom-call | tf_op jit(solution)/shard_map/transition/pallas_call | solution.py:332
  23.3 0.0 all-to-all-done.1
  23.3 7.1 %all-to-all-start = ((f32[32,64,128]{2,1,0:T(8,128)}), f32[32,64,128]{2,1,0:T(8,128)S(1)}, u32[]{:S(2)}, u32[]{:S(2)}) async-start(f32[32,64,128]{2,1,0:T(8,128)} %bitcast.31), calls=%async_computation | async-start | bytes 2097152 | tf_op jit(solution)/shard_map/all_to_all | solution.py:356
  30.4 3.7 %collective-permute-start.8 = (f32[128,128]{1,0:T(8,128)S(1)}, f32[128,128]{1,0:T(8,128)S(1)}, u32[]{:S(2)}, u32[]{:S(2)}) collective-permute-start(f32[128,128]{1,0:T(8,128)S(1)} %constant_dynamic-slice_fusion), channel_id=1, source_target_pairs={{0,0},{1,1},{2,2},{3,3},{4,32},{5,33},{6,34},{7,35},{8,64},{9,65},... | collective-permute-start | bytes 196616 | tf_op jit(solution)/shard_map/ppermute | solution.py:362
  34.1 0.7 copy.17.wb_ref
  34.9 4.6 %bias.1.bias_ref = f32[128,512]{1,0:T(8,128)} custom-call(f32[4096,128]{1,0:T(8,128)} %bitcast.29, f32[128,16]{1,0:T(8,128)} %copy.17.wb_ref), custom_call_target="tpu_custom_call" | custom-call | tf_op jit(solution)/shard_map/bias/pallas_call | solution.py:364
  39.5 0.6 copy-done.10
  40.1 4.1 %attention.1 = (f32[512,128]{1,0:T(8,128)}, f32[64,128]{1,0:T(8,128)}, f32[32,128]{1,0:T(8,128)}) custom-call(f32[512,128]{1,0:T(8,128)} %bitcast.36, f32[128,128]{1,0:T(8,128)} %copy-done.10, f32[128,512]{1,0:T(8,128)} %bias.1.bias_ref, f32[384,384]{1,0:T(8,128)} %wq_ref.1, f32[384,384]{1,0:T(8,128)} %wk_ref.1, f32[384,384]{1,0:T(8,128)} %wv_ref.1), custom_call_target="tpu_custom_call" | custom-call | tf_op jit(solution)/shard_map/attention/pallas_call | solution.py:383
  44.2 5.5 %all-to-all-done = f32[32,64,128]{2,1,0:T(8,128)S(1)} async-done(((f32[32,64,128]{2,1,0:T(8,128)}), f32[32,64,128]{2,1,0:T(8,128)S(1)}, u32[]{:S(2)}, u32[]{:S(2)}) %all-to-all-start) | async-done | bytes 1048608 | tf_op jit(solution)/shard_map/all_to_all | solution.py:356
  49.7 8.3 %all-to-all-start.2 = ((f32[32,16,128]{2,1,0:T(8,128)}), f32[32,16,128]{2,1,0:T(8,128)S(1)}, u32[]{:S(2)}, u32[]{:S(2)}) async-start(f32[32,16,128]{2,1,0:T(8,128)} %bitcast.38), calls=%async_computation.2 | async-start | bytes 524288 | tf_op jit(solution)/shard_map/all_to_all | solution.py:402
  58.1 0.1 dynamic-slice_bitcast_fusion
  58.2 6.0 %collective-permute-start.7 = (f32[4,64,128]{2,1,0:T(8,128)S(1)}, f32[4,64,128]{2,1,0:T(8,128)S(1)}, u32[]{:S(2)}, u32[]{:S(2)}) collective-permute-start(f32[4,64,128]{2,1,0:T(8,128)S(1)} %get-tuple-element.16), channel_id=1, source_target_pairs={{0,56},{1,57},{2,58},{3,59},{4,24},{5,25},{6,26},{7,27},{8,120},{9... | collective-permute-start | bytes 393224 | tf_op jit(solution)/shard_map/ppermute | solution.py:399
  64.2 0.5 collective-permute-start.6
  64.7 3.4 %collective-permute-start.5 = (f32[4,64,128]{2,1,0:T(8,128)S(1)}, f32[4,64,128]{2,1,0:T(8,128)S(1)}, u32[]{:S(2)}, u32[]{:S(2)}) collective-permute-start(f32[4,64,128]{2,1,0:T(8,128)S(1)} %get-tuple-element.18), channel_id=1, source_target_pairs={{0,48},{1,49},{2,50},{3,51},{4,16},{5,17},{6,18},{7,19},{8,112},{9... | collective-permute-start | bytes 393224 | tf_op jit(solution)/shard_map/ppermute | solution.py:399
  68.1 2.7 %collective-permute-start.4 = (f32[4,64,128]{2,1,0:T(8,128)S(1)}, f32[4,64,128]{2,1,0:T(8,128)S(1)}, u32[]{:S(2)}, u32[]{:S(2)}) collective-permute-start(f32[4,64,128]{2,1,0:T(8,128)S(1)} %get-tuple-element.19), channel_id=1, source_target_pairs={{0,16},{1,17},{2,18},{3,19},{4,48},{5,49},{6,50},{7,51},{8,80},{9,... | collective-permute-start | bytes 393224 | tf_op jit(solution)/shard_map/ppermute | solution.py:399
  70.8 4.0 %collective-permute-start.3 = (f32[4,64,128]{2,1,0:T(8,128)S(1)}, f32[4,64,128]{2,1,0:T(8,128)S(1)}, u32[]{:S(2)}, u32[]{:S(2)}) collective-permute-start(f32[4,64,128]{2,1,0:T(8,128)S(1)} %get-tuple-element.20), channel_id=1, source_target_pairs={{0,40},{1,41},{2,42},{3,43},{4,8},{5,9},{6,10},{7,11},{8,104},{9,1... | collective-permute-start | bytes 393224 | tf_op jit(solution)/shard_map/ppermute | solution.py:399
  74.8 4.4 %collective-permute-done.7.refs_7_ = f32[4,64,128]{2,1,0:T(8,128)S(1)} collective-permute-done((f32[4,64,128]{2,1,0:T(8,128)S(1)}, f32[4,64,128]{2,1,0:T(8,128)S(1)}, u32[]{:S(2)}, u32[]{:S(2)}) %collective-permute-start.7) | collective-permute-done | bytes 131104 | tf_op jit(solution)/shard_map/ppermute | solution.py:399
  79.1 3.5 %collective-permute-done.6.refs_6_ = f32[4,64,128]{2,1,0:T(8,128)S(1)} collective-permute-done((f32[4,64,128]{2,1,0:T(8,128)S(1)}, f32[4,64,128]{2,1,0:T(8,128)S(1)}, u32[]{:S(2)}, u32[]{:S(2)}) %collective-permute-start.6) | collective-permute-done | bytes 131104 | tf_op jit(solution)/shard_map/ppermute | solution.py:399
  82.7 4.3 %collective-permute-start.1 = (f32[4,64,128]{2,1,0:T(8,128)S(1)}, f32[4,64,128]{2,1,0:T(8,128)S(1)}, u32[]{:S(2)}, u32[]{:S(2)}) collective-permute-start(f32[4,64,128]{2,1,0:T(8,128)S(1)} %get-tuple-element.22), channel_id=1, source_target_pairs={{0,32},{1,33},{2,34},{3,35},{4,0},{5,1},{6,2},{7,3},{8,96},{9,97},... | collective-permute-start | bytes 393224 | tf_op jit(solution)/shard_map/ppermute | solution.py:399
  87.0 5.9 %collective-permute-done.5.refs_5_ = f32[4,64,128]{2,1,0:T(8,128)S(1)} collective-permute-done((f32[4,64,128]{2,1,0:T(8,128)S(1)}, f32[4,64,128]{2,1,0:T(8,128)S(1)}, u32[]{:S(2)}, u32[]{:S(2)}) %collective-permute-start.5) | collective-permute-done | bytes 131104 | tf_op jit(solution)/shard_map/ppermute | solution.py:399
  92.9 1.9 %collective-permute-start = (f32[4,64,128]{2,1,0:T(8,128)S(1)}, f32[4,64,128]{2,1,0:T(8,128)S(1)}, u32[]{:S(2)}, u32[]{:S(2)}) collective-permute-start(f32[4,64,128]{2,1,0:T(8,128)S(1)} %get-tuple-element.23), channel_id=1, source_target_pairs={{0,0},{1,1},{2,2},{3,3},{4,32},{5,33},{6,34},{7,35},{8,64},{9,65},... | collective-permute-start | bytes 393224 | tf_op jit(solution)/shard_map/ppermute | solution.py:399
  94.8 3.9 %own.1 = (f32[64,32,128]{2,1,0:T(8,128)}, bf16[64,32,128]{2,1,0:T(8,128)(2,1)}) custom-call(f32[8,4,4,16,128]{4,3,2,1,0:T(8,128)} %get-tuple-element.9.proj_ref, f32[1,64]{1,0:T(1,128)} %bitcast.42), custom_call_target="tpu_custom_call" | custom-call | tf_op jit(solution)/shard_map/own/pallas_call | solution.py:374
  98.8 0.7 copy-done.1
  99.5 2.8 %merge.1 = f32[4,384]{1,0:T(4,128)} custom-call(f32[512,128]{1,0:T(8,128)} %bitcast.37, f32[4,384]{1,0:T(4,128)} %single_ref.3, f32[384,384]{1,0:T(8,128)} %wg_ref.3, f32[384,384]{1,0:T(8,128)} %wo_ref.3), custom_call_target="tpu_custom_call" | custom-call | tf_op jit(solution)/shard_map/merge/pallas_call | solution.py:404
  102.3 0.0 collective-permute-done.3.refs_3_
  102.3 0.0 collective-permute-done.2.refs_2_
  102.3 5.2 %collective-permute-done.refs_0_ = f32[4,64,128]{2,1,0:T(8,128)S(1)} collective-permute-done((f32[4,64,128]{2,1,0:T(8,128)S(1)}, f32[4,64,128]{2,1,0:T(8,128)S(1)}, u32[]{:S(2)}, u32[]{:S(2)}) %collective-permute-start) | collective-permute-done | bytes 131104 | tf_op jit(solution)/shard_map/ppermute | solution.py:399
  107.6 0.6 copy-done.9
  108.2 5.5 %gradient.1 = f32[4,2,16,32,128]{4,3,2,1,0:T(8,128)} custom-call(s32[1]{0:T(128)} %bitcast.place_ref, f32[4,64,128]{2,1,0:T(8,128)} %copy-done.9, f32[4,64,128]{2,1,0:T(8,128)} %copy-done.8, f32[4,64,128]{2,1,0:T(8,128)} %copy-done.7, f32[4,64,128]{2,1,0:T(8,128)} %copy-done.6, f32[4,64,128]{2,1,0:T(8,128)} %copy-done.5, f32[4,64,128]{2,1,0:T(8,128)} %copy-done.4, ...), custom_call_target="tpu_custom_call" | custom-call | tf_op jit(solution)/shard_map/gradient/pallas_call | solution.py:409
  (26 shorter events, 0.1 us)
Async XLA Ops:
  2.2 21.1 %all-to-all-start.1 = ((f32[32,16,128]{2,1,0:T(8,128)}), f32[32,16,128]{2,1,0:T(8,128)S(1)}, u32[]{:S(2)}, u32[]{:S(2)}) async-start(f32[32,16,128]{2,1,0:T(8,128)} %tokens.1), calls=%async_computation.1 | async-start | bytes 524288 | tf_op jit(solution)/shard_map/all_to_all | solution.py:329
  11.0 23.2 %copy-start.11 = (f32[128,16]{0,1:T(8,128)S(1)}, f32[128,16]{0,1:T(8,128)}, u32[]{:S(2)}) copy-start(f32[128,16]{0,1:T(8,128)} %param.22) | copy-start | bytes 24580
  23.3 16.2 %copy-start = (f32[32,16,128]{2,1,0:T(8,128)}, f32[32,16,128]{2,1,0:T(8,128)S(1)}, u32[]{:S(2)}) copy-start(f32[32,16,128]{2,1,0:T(8,128)S(1)} %all-to-all-done.1) | copy-start | bytes 786436
  23.3 26.4 %all-to-all-start = ((f32[32,64,128]{2,1,0:T(8,128)}), f32[32,64,128]{2,1,0:T(8,128)S(1)}, u32[]{:S(2)}, u32[]{:S(2)}) async-start(f32[32,64,128]{2,1,0:T(8,128)} %bitcast.31), calls=%async_computation | async-start | bytes 2097152 | tf_op jit(solution)/shard_map/all_to_all | solution.py:356
  30.4 9.1 %collective-permute-start.8 = (f32[128,128]{1,0:T(8,128)S(1)}, f32[128,128]{1,0:T(8,128)S(1)}, u32[]{:S(2)}, u32[]{:S(2)}) collective-permute-start(f32[128,128]{1,0:T(8,128)S(1)} %constant_dynamic-slice_fusion), channel_id=1, source_target_pairs={{0,0},{1,1},{2,2},{3,3},{4,32},{5,33},{6,34},{7,35},{8,64},{9,65},... | collective-permute-start | bytes 196616 | tf_op jit(solution)/shard_map/ppermute | solution.py:362
  39.5 0.6 copy-start.10
  49.7 49.1 %all-to-all-start.2 = ((f32[32,16,128]{2,1,0:T(8,128)}), f32[32,16,128]{2,1,0:T(8,128)S(1)}, u32[]{:S(2)}, u32[]{:S(2)}) async-start(f32[32,16,128]{2,1,0:T(8,128)} %bitcast.38), calls=%async_computation.2 | async-start | bytes 524288 | tf_op jit(solution)/shard_map/all_to_all | solution.py:402
  58.2 20.9 %collective-permute-start.7 = (f32[4,64,128]{2,1,0:T(8,128)S(1)}, f32[4,64,128]{2,1,0:T(8,128)S(1)}, u32[]{:S(2)}, u32[]{:S(2)}) collective-permute-start(f32[4,64,128]{2,1,0:T(8,128)S(1)} %get-tuple-element.16), channel_id=1, source_target_pairs={{0,56},{1,57},{2,58},{3,59},{4,24},{5,25},{6,26},{7,27},{8,120},{9... | collective-permute-start | bytes 393224 | tf_op jit(solution)/shard_map/ppermute | solution.py:399
  64.2 18.5 %collective-permute-start.6 = (f32[4,64,128]{2,1,0:T(8,128)S(1)}, f32[4,64,128]{2,1,0:T(8,128)S(1)}, u32[]{:S(2)}, u32[]{:S(2)}) collective-permute-start(f32[4,64,128]{2,1,0:T(8,128)S(1)} %get-tuple-element.17), channel_id=1, source_target_pairs={{0,24},{1,25},{2,26},{3,27},{4,56},{5,57},{6,58},{7,59},{8,88},{9,... | collective-permute-start | bytes 393224 | tf_op jit(solution)/shard_map/ppermute | solution.py:399
  64.7 28.2 %collective-permute-start.5 = (f32[4,64,128]{2,1,0:T(8,128)S(1)}, f32[4,64,128]{2,1,0:T(8,128)S(1)}, u32[]{:S(2)}, u32[]{:S(2)}) collective-permute-start(f32[4,64,128]{2,1,0:T(8,128)S(1)} %get-tuple-element.18), channel_id=1, source_target_pairs={{0,48},{1,49},{2,50},{3,51},{4,16},{5,17},{6,18},{7,19},{8,112},{9... | collective-permute-start | bytes 393224 | tf_op jit(solution)/shard_map/ppermute | solution.py:399
  68.1 34.2 %collective-permute-start.4 = (f32[4,64,128]{2,1,0:T(8,128)S(1)}, f32[4,64,128]{2,1,0:T(8,128)S(1)}, u32[]{:S(2)}, u32[]{:S(2)}) collective-permute-start(f32[4,64,128]{2,1,0:T(8,128)S(1)} %get-tuple-element.19), channel_id=1, source_target_pairs={{0,16},{1,17},{2,18},{3,19},{4,48},{5,49},{6,50},{7,51},{8,80},{9,... | collective-permute-start | bytes 393224 | tf_op jit(solution)/shard_map/ppermute | solution.py:399
  70.8 31.5 %collective-permute-start.3 = (f32[4,64,128]{2,1,0:T(8,128)S(1)}, f32[4,64,128]{2,1,0:T(8,128)S(1)}, u32[]{:S(2)}, u32[]{:S(2)}) collective-permute-start(f32[4,64,128]{2,1,0:T(8,128)S(1)} %get-tuple-element.20), channel_id=1, source_target_pairs={{0,40},{1,41},{2,42},{3,43},{4,8},{5,9},{6,10},{7,11},{8,104},{9,1... | collective-permute-start | bytes 393224 | tf_op jit(solution)/shard_map/ppermute | solution.py:399
  79.1 28.4 %copy-start.2 = (f32[4,64,128]{2,1,0:T(8,128)}, f32[4,64,128]{2,1,0:T(8,128)S(1)}, u32[]{:S(2)}) copy-start(f32[4,64,128]{2,1,0:T(8,128)S(1)} %collective-permute-done.7.refs_7_) | copy-start | bytes 393220
  79.1 23.1 %collective-permute-start.2 = (f32[4,64,128]{2,1,0:T(8,128)S(1)}, f32[4,64,128]{2,1,0:T(8,128)S(1)}, u32[]{:S(2)}, u32[]{:S(2)}) collective-permute-start(f32[4,64,128]{2,1,0:T(8,128)S(1)} %get-tuple-element.21), channel_id=1, source_target_pairs={{0,8},{1,9},{2,10},{3,11},{4,40},{5,41},{6,42},{7,43},{8,72},{9,73... | collective-permute-start | bytes 393224 | tf_op jit(solution)/shard_map/ppermute | solution.py:399
  82.7 24.9 %copy-start.3 = (f32[4,64,128]{2,1,0:T(8,128)}, f32[4,64,128]{2,1,0:T(8,128)S(1)}, u32[]{:S(2)}) copy-start(f32[4,64,128]{2,1,0:T(8,128)S(1)} %collective-permute-done.6.refs_6_) | copy-start | bytes 393220
  82.7 19.6 %collective-permute-start.1 = (f32[4,64,128]{2,1,0:T(8,128)S(1)}, f32[4,64,128]{2,1,0:T(8,128)S(1)}, u32[]{:S(2)}, u32[]{:S(2)}) collective-permute-start(f32[4,64,128]{2,1,0:T(8,128)S(1)} %get-tuple-element.22), channel_id=1, source_target_pairs={{0,32},{1,33},{2,34},{3,35},{4,0},{5,1},{6,2},{7,3},{8,96},{9,97},... | collective-permute-start | bytes 393224 | tf_op jit(solution)/shard_map/ppermute | solution.py:399
  92.9 14.6 %copy-start.4 = (f32[4,64,128]{2,1,0:T(8,128)}, f32[4,64,128]{2,1,0:T(8,128)S(1)}, u32[]{:S(2)}) copy-start(f32[4,64,128]{2,1,0:T(8,128)S(1)} %collective-permute-done.5.refs_5_) | copy-start | bytes 393220
  92.9 14.6 %collective-permute-start = (f32[4,64,128]{2,1,0:T(8,128)S(1)}, f32[4,64,128]{2,1,0:T(8,128)S(1)}, u32[]{:S(2)}, u32[]{:S(2)}) collective-permute-start(f32[4,64,128]{2,1,0:T(8,128)S(1)} %get-tuple-element.23), channel_id=1, source_target_pairs={{0,0},{1,1},{2,2},{3,3},{4,32},{5,33},{6,34},{7,35},{8,64},{9,65},... | collective-permute-start | bytes 393224 | tf_op jit(solution)/shard_map/ppermute | solution.py:399
  98.8 0.7 copy-start.1
  102.2 5.3 %copy-start.5 = (f32[4,64,128]{2,1,0:T(8,128)}, f32[4,64,128]{2,1,0:T(8,128)S(1)}, u32[]{:S(2)}) copy-start(f32[4,64,128]{2,1,0:T(8,128)S(1)} %collective-permute-done.4.refs_4_) | copy-start | bytes 393220
  102.3 5.3 %copy-start.6 = (f32[4,64,128]{2,1,0:T(8,128)}, f32[4,64,128]{2,1,0:T(8,128)S(1)}, u32[]{:S(2)}) copy-start(f32[4,64,128]{2,1,0:T(8,128)S(1)} %collective-permute-done.3.refs_3_) | copy-start | bytes 393220
  102.3 5.3 %copy-start.7 = (f32[4,64,128]{2,1,0:T(8,128)}, f32[4,64,128]{2,1,0:T(8,128)S(1)}, u32[]{:S(2)}) copy-start(f32[4,64,128]{2,1,0:T(8,128)S(1)} %collective-permute-done.2.refs_2_) | copy-start | bytes 393220
  102.3 5.3 %copy-start.8 = (f32[4,64,128]{2,1,0:T(8,128)}, f32[4,64,128]{2,1,0:T(8,128)S(1)}, u32[]{:S(2)}) copy-start(f32[4,64,128]{2,1,0:T(8,128)S(1)} %collective-permute-done.1.refs_1_) | copy-start | bytes 393220
  107.5 0.6 copy-start.9
where the time goes:
time: 114 us
  starting transfers between devices  50.7 us (44%)
  Pallas kernels  34.7 us (30%)
  waiting for transfers between devices  24.5 us (21%)
  local copies, waits for them, and re-layouts  2.79 us (2%)
    ppermute x8, starting transfers between devices, per_device(): parts.append(lax.ppermute(piece, ALL, perm))  22.8 us
    ppermute x8, waiting for transfers between devices, per_device(): parts.append(lax.ppermute(piece, ALL, perm))  19 us
    pallas_call x1, Pallas kernels, per_device(): pl.pallas_call(transition_kernel, grid=(4,), in_specs=[pl.BlockSpec((4, 2...  12.3 us
    all_to_all x1, starting transfers between devices, per_device(): rows_tok = lax.all_to_all(tok, COL, split_axis=0, concat_axis=0, tiled=True)  8.79 us
    all_to_all x1, starting transfers between devices, per_device(): lax.all_to_all(msg.reshape(32, 16, 128), COL, split_axis=0, concat_axis=0...  8.34 us
    all_to_all x1, starting transfers between devices, per_device(): lax.all_to_all(proj.reshape(32, 64, 128), PLANE, split_axis=0, concat_axi...  7.1 us
    all_to_all x1, waiting for transfers between devices, per_device(): lax.all_to_all(proj.reshape(32, 64, 128), PLANE, split_axis=0, concat_axi...  5.51 us
    pallas_call x1, Pallas kernels, per_device(): pl.pallas_call(gradient_kernel, grid_spec=pltpu.PrefetchScalarGridSpec(nu...  5.49 us
  transfers between devices with their start and end apart: 12, of which 5 were waited for; matrix products, arithmetic and copies ran while one was open for 1% of the time, Pallas kernels for 24%

commit v1 on v0

--- a/solution.py
+++ b/solution.py
@@ -77,7 +77,20 @@
 
 
 def transition_kernel(
-    pair_ref, tt_ref, wg_ref, wu_ref, wo_ref, wdt_ref, mid_ref, proj_ref, w1_ref, w2_ref, wp_ref
+    pair_ref,
+    tt_ref,
+    wg_ref,
+    wu_ref,
+    wo_ref,
+    wdt_ref,
+    bd_ref,
+    mid_ref,
+    proj_ref,
+    own_ref,
+    hits_ref,
+    w1_ref,
+    w2_ref,
+    wp_ref,
 ):
     step = pl.program_id(0)
 
@@ -103,20 +116,36 @@
         o = mm(hh, w2_ref[c : c + 256, :])
         out = out + (o[:, :128] + (o[:, 128:] + mm(hl, w2_ref[c : c + 256, :128])))
     mid = x + out
-    mid_ref[...] = mid.reshape(4, 2, 4, 32, 128)
+    mid_ref[...] = mid.reshape(4, 2, 1, 4, 32, 128)
     split = mid.reshape(32, 2, 16, 128)
     proj = project(split[:, 0].reshape(512, 128), split[:, 1].reshape(512, 128), wp_ref)
-    turned = pltpu.roll(tt_ref[...].astype(F32), (128 - 8 * step) % 128, 1)
+    turned = pltpu.roll(tt_ref[...].astype(F32), (128 - 4 * step) % 128, 1)
     lane = lanes_of((16, 128))
+    left = lane < 64
+    at_zero = lane % 64 == 0
+    number = (lane % 64).astype(F32)
+    bd = bd_ref[...]
+    bd = bd - bd[:, 0:1]
+    bd = jnp.concatenate([bd, bd], axis=1)
     for k in range(4):
-        for st in range(2):
-            for w in range(4):
-                i = k * 32 + st * 4 + w
-                a = turned[0:16, i : i + 1]
-                b = turned[16:32, i : i + 1]
-                mark = jnp.where(lane == 0, a, jnp.where(lane == 64, b, 0.0))
-                n = (k * 8 + st * 4 + w) * 16
-                proj_ref[st, k, w] = proj[n : n + 16] + mark
+        for w in range(4):
+            tile, front, back = [], [], []
+            for ih in range(2):
+                i = k * 32 + ih * 16 + w
+                a = jnp.broadcast_to(turned[0:16, i : i + 1], (16, 128))
+                b = jnp.broadcast_to(turned[16:32, i : i + 1], (16, 128))
+                n = (k * 8 + ih * 4 + w) * 16
+                p = proj[n : n + 16]
+                proj_ref[ih, 0, k, w] = jnp.where(at_zero, jnp.where(left, a, b), p)
+                tile.append(p)
+                front.append(a)
+                back.append(b)
+            own_ref[k, 0, w, 0:16] = jnp.where(left, tile[0], pltpu.roll(tile[1], 64, 1)) + bd
+            own_ref[k, 0, w, 16:32] = jnp.where(left, pltpu.roll(tile[0], 64, 1), tile[1]) + bd
+            hit = [
+                jnp.where(number == jnp.where(left, t[0], t[1]), 1.0, 0.0) for t in (front, back)
+            ]
+            hits_ref[k, 0, w] = jnp.concatenate(hit, axis=0).astype(BF16)
 
 
 def bias_kernel(mid_ref, wb_ref, bias_ref, w3_ref, n_ref):
@@ -147,26 +176,22 @@
     return jnp.where((row // 64 == lanes_of((128, 128)) // 64) & (row % 64 == 0), 1.0, 0.0).astype(BF16)
 
 
-def own_kernel(proj_ref, bd_ref, own_ref, hits_ref):
-    front = proj_ref[0:4, 0].reshape(256, 128)
-    back = proj_ref[4:8, 0].reshape(256, 128)
-    left = lanes_of((256, 128)) < 64
-    own_a = jnp.where(left, front, pltpu.roll(back, 64, 1)).reshape(16, 16, 128)
-    own_b = jnp.where(left, pltpu.roll(front, 64, 1), back).reshape(16, 16, 128)
-    own = jnp.concatenate([own_a, own_b], axis=1).reshape(512, 128)
-    bins = lanes_of((512, 128)) % 64
-    mark = jnp.where(bins == 0, own, 0.0)
-    target = mm(mark.astype(BF16), pick_matrix())
-    bd = bd_ref[...]
-    bd = bd - bd[:, 0:1]
-    own_ref[...] = (own - mark + jnp.concatenate([bd, bd], axis=1)).reshape(16, 32, 128)
-    hits = jnp.where(bins.astype(F32) == target, 1.0, 0.0).astype(BF16)
-    hits_ref[...] = hits.reshape(16, 32, 128)
-
-
 def attention_kernel(
-    xr_ref, xc_ref, bias_ref, wq_ref, wk_ref, wv_ref, msg_ref, rowpad_ref, colpad_ref
+    xr_ref,
+    xc_ref,
+    bias_ref,
+    wq_ref,
+    wk_ref,
+    wv_ref,
+    single_ref,
+    wg_ref,
+    msg_ref,
+    rowpad_ref,
+    colpad_ref,
+    gate_ref,
 ):
+    gate_ref[...] = 1.0 / (1.0 + jnp.exp(-mm3(norm(single_ref[...]), wg_ref[...])))
+
     def tokens(ref, n):
         x = jnp.concatenate([ref[pl.ds(q, n, stride=4), :] for q in range(3)], axis=1)
         return norm(x), ref[pl.ds(3, n, stride=4), :][:, 0:1]
@@ -209,7 +234,7 @@
     msg_ref[pl.ds(3, 128, stride=4), :] = tail
 
 
-def merge_kernel(msg_ref, single_ref, wg_ref, wo_ref, out_ref):
+def merge_tokens(msg_ref, single_ref, gate_ref, wo_ref, out_ref):
     lane = lanes_of((32, 128))
     accs, factors, totals = [], [], []
     for t in range(4):
@@ -231,15 +256,14 @@
         num = jnp.sum(wide[t * 32 : (t + 1) * 32] * accs[t], axis=0, keepdims=True)
         rows.append(num / wide[128 + t : 129 + t])
     attended = jnp.concatenate(rows, axis=0)
-    single = single_ref[...]
-    g = mm3(norm(single), wg_ref[...])
-    out_ref[...] = single + mm3(attended / (1.0 + jnp.exp(-g)), wo_ref[...])
+    out_ref[...] = single_ref[...] + mm3(gate_ref[...] * attended, wo_ref[...])
 
 
 def gradient_kernel(place_ref, *refs):
     parts = refs[:8]
-    own_ref, hits_ref, mid_ref, rowpad_ref, colpad_ref, wdt_ref, out_ref = refs[8:15]
-    f_ref, w_ref, ones_ref, pick_ref, d_ref = refs[15:]
+    own_ref, hits_ref, mid_ref, rowpad_ref, colpad_ref, wdt_ref = refs[8:14]
+    msg_ref, single_ref, gate_ref, wo_ref, out_ref, single_out_ref = refs[14:20]
+    f_ref, w_ref, ones_ref, pick_ref, d_ref = refs[20:]
 
     @pl.when(pl.program_id(0) == 0)
     def _():
@@ -279,6 +303,10 @@
     change = mm(d_ref[...], w_ref[0]) + mm(d_ref[...], w_ref[1])
     for k in range(2):
         out_ref[0, k] = mid_ref[0, k] + change[:, k * 128 : (k + 1) * 128].reshape(16, 32, 128)
+
+    @pl.when(pl.program_id(0) == 3)
+    def _():
+        merge_tokens(msg_ref, single_ref, gate_ref, wo_ref, single_out_ref)
 
 
 def tokens_kernel(single_ref, pad_ref, out_ref):
@@ -329,29 +357,37 @@
     rows_tok = lax.all_to_all(tok, COL, split_axis=0, concat_axis=0, tiled=True)
     rows_tok = rows_tok.reshape(512, 128)
 
-    mid, proj = pl.pallas_call(
+    mid, proj, own, hits = pl.pallas_call(
         transition_kernel,
         grid=(4,),
         in_specs=[
-            pl.BlockSpec((4, 2, 4, 32, 128), lambda s: (0, s, 0, 0, 0)),
+            pl.BlockSpec((4, 2, 1, 4, 32, 128), lambda s: (0, 0, s, 0, 0, 0)),
             full((32, 128)),
             full((128, 512)),
             full((128, 512)),
             full((512, 128)),
             full((64, 128)),
+            full((1, 64)),
         ],
         out_specs=[
-            pl.BlockSpec((4, 2, 4, 32, 128), lambda s: (0, s, 0, 0, 0)),
-            pl.BlockSpec((2, 4, 4, 16, 128), lambda s: (s, 0, 0, 0, 0)),
+            pl.BlockSpec((4, 2, 1, 4, 32, 128), lambda s: (0, 0, s, 0, 0, 0)),
+            pl.BlockSpec((2, 1, 4, 4, 16, 128), lambda s: (0, s, 0, 0, 0, 0)),
+            pl.BlockSpec((4, 1, 4, 32, 128), lambda s: (0, s, 0, 0, 0)),
+            pl.BlockSpec((4, 1, 4, 32, 128), lambda s: (0, s, 0, 0, 0)),
         ],
-        out_shape=[struct(4, 8, 4, 32, 128), struct(8, 4, 4, 16, 128)],
+        out_shape=[
+            struct(4, 2, 4, 4, 32, 128),
+            struct(2, 4, 4, 4, 16, 128),
+            struct(4, 4, 4, 32, 128),
+            jax.ShapeDtypeStruct((4, 4, 4, 32, 128), BF16),
+        ],
         scratch_shapes=[
             pltpu.VMEM((2, 2, 256, 512), BF16),
             pltpu.VMEM((512, 256), BF16),
             pltpu.VMEM((256, 256), BF16),
         ],
         name="transition",
-    )(pair.reshape(4, 8, 4, 32, 128), tt, w_gate, w_up, w_out, wdt)
+    )(pair.reshape(4, 2, 4, 4, 32, 128), tt, w_gate, w_up, w_out, wdt, b_dist[None])
 
     spread = lax.all_to_all(
         proj.reshape(32, 64, 128), PLANE, split_axis=0, concat_axis=0, tiled=True
@@ -371,20 +407,11 @@
         name="bias",
     )(mid.reshape(4096, 128), w_bias)
 
-    own, hits = pl.pallas_call(
-        own_kernel,
-        grid=(4,),
-        in_specs=[pl.BlockSpec((8, 1, 4, 16, 128), lambda m: (0, m, 0, 0, 0)), full((1, 64))],
-        out_specs=[pl.BlockSpec((16, 32, 128), lambda m: (m, 0, 0))] * 2,
-        out_shape=[struct(64, 32, 128), jax.ShapeDtypeStruct((64, 32, 128), BF16)],
-        name="own",
-    )(proj, b_dist[None])
-
-    msg, rowpad, colpad = pl.pallas_call(
+    msg, rowpad, colpad, gate = pl.pallas_call(
         attention_kernel,
-        out_shape=[struct(512, 128), struct(64, 128), struct(32, 128)],
+        out_shape=[struct(512, 128), struct(64, 128), struct(32, 128), struct(4, 384)],
         name="attention",
-    )(rows_tok, cols_tok, bias, w_query, w_key, w_value)
+    )(rows_tok, cols_tok, bias, w_query, w_key, w_value, single, w_gating)
 
     parts = []
     for n in range(8):
@@ -401,12 +428,8 @@
 
     merged = lax.all_to_all(msg.reshape(32, 16, 128), COL, split_axis=0, concat_axis=0, tiled=True)
     merged = merged.reshape(512, 128)
-    single_out = pl.pallas_call(
-        merge_kernel, out_shape=struct(4, 384), name="merge"
-    )(merged, single, w_gating, w_attn_out)
-
     grouped = pl.BlockSpec((1, 2, 16, 32, 128), lambda m, _: (m, 0, 0, 0, 0))
-    pair_out = pl.pallas_call(
+    pair_out, single_out = pl.pallas_call(
         gradient_kernel,
         grid_spec=pltpu.PrefetchScalarGridSpec(
             num_scalar_prefetch=1,
@@ -419,8 +442,12 @@
                 pl.BlockSpec((16, 128), lambda m, _: (m, 0)),
                 full((32, 128)),
                 full((64, 128)),
+                full((512, 128)),
+                full((4, 384)),
+                full((4, 384)),
+                full((384, 384)),
             ],
-            out_specs=grouped,
+            out_specs=[grouped, full((4, 384))],
             scratch_shapes=[
                 pltpu.VMEM((512, 128), F32),
                 pltpu.VMEM((2, 256, 256), BF16),
@@ -429,17 +456,21 @@
                 pltpu.VMEM((512, 256), BF16),
             ],
         ),
-        out_shape=struct(4, 2, 16, 32, 128),
+        out_shape=[struct(4, 2, 16, 32, 128), struct(4, 384)],
         name="gradient",
     )(
         place,
         *parts,
-        own,
-        hits,
+        own.reshape(64, 32, 128),
+        hits.reshape(64, 32, 128),
         mid.reshape(4, 2, 16, 32, 128),
         rowpad,
         colpad,
         wdt,
+        merged,
+        single,
+        gate,
+        w_attn_out,
     )
     pair_out = pair_out.reshape(128, 32, 128)
     return (pair_out, single_out)

time: 114 us -> 116 us (1.018)
  waiting for transfers between devices: 24.5 us -> 32 us
  Pallas kernels: 34.7 us -> 29.9 us
    ppermute x8, waiting for transfers between devices: 19 us -> 26.8 us  [per_device(): parts.append(lax.ppermute(piece, ALL, perm))]
    pallas_call x2 -> x0, Pallas kernels: 6.71 us -> none  [the longest x1 3.93 us: per_device(): pl.pallas_call(own_kernel, grid=(4,), in_specs=[pl.BlockSpec((8, 1, 4, 16...]
  transfers between devices with their start and end apart: 12 -> 12, of which waited for: 5 -> 5; matrix products, arithmetic and copies ran while one was open for 1% -> 1% of each run, Pallas kernels for 24% -> 19%
where the time goes in v1:
time: 116 us
  starting transfers between devices  50.7 us (44%)
  waiting for transfers between devices  32 us (28%)
  Pallas kernels  29.9 us (26%)
  local copies, waits for them, and re-layouts  2.1 us (2%)
    ppermute x8, waiting for transfers between devices, per_device(): parts.append(lax.ppermute(piece, ALL, perm))  26.8 us
    ppermute x8, starting transfers between devices, per_device(): parts.append(lax.ppermute(piece, ALL, perm))  22.7 us
    pallas_call x1, Pallas kernels, per_device(): pl.pallas_call(transition_kernel, grid=(4,), in_specs=[pl.BlockSpec((4, 2...  12.8 us
    all_to_all x1, starting transfers between devices, per_device(): rows_tok = lax.all_to_all(tok, COL, split_axis=0, concat_axis=0, tiled=True)  8.79 us
    all_to_all x1, starting transfers between devices, per_device(): lax.all_to_all(msg.reshape(32, 16, 128), COL, split_axis=0, concat_axis=0...  8.34 us
    all_to_all x1, starting transfers between devices, per_device(): lax.all_to_all(proj.reshape(32, 64, 128), PLANE, split_axis=0, concat_axi...  7.09 us
    pallas_call x1, Pallas kernels, per_device(): pl.pallas_call(gradient_kernel, grid_spec=pltpu.PrefetchScalarGridSpec(nu...  6.61 us
    all_to_all x1, waiting for transfers between devices, per_device(): lax.all_to_all(proj.reshape(32, 64, 128), PLANE, split_axis=0, concat_axi...  5.25 us
  transfers between devices with their start and end apart: 12, of which 5 were waited for; matrix products, arithmetic and copies ran while one was open for 1% of the time, Pallas kernels for 19%

profile of v1, /device:TPU:32, one launch (start us, length us, event | category | flops | bytes accessed | tf_op | source)
XLA Modules:
  0.0 115.6 jit_solution(15635652013549070525)
XLA Ops:
  0.6 1.5 %tokens.1 = f32[32,16,128]{2,1,0:T(8,128)} custom-call(f32[4,384]{1,0:T(4,128)} %refs_15_.1, s32[4]{0:T(128)} %pad_ref.1), custom_call_target="tpu_custom_call" | custom-call | tf_op jit(solution)/shard_map/tokens/pallas_call | solution.py:351
  2.1 8.8 %all-to-all-start.1 = ((f32[32,16,128]{2,1,0:T(8,128)}), f32[32,16,128]{2,1,0:T(8,128)S(1)}, u32[]{:S(2)}, u32[]{:S(2)}) async-start(f32[32,16,128]{2,1,0:T(8,128)} %tokens.1), calls=%async_computation.1 | async-start | bytes 524288 | tf_op jit(solution)/shard_map/all_to_all | solution.py:357
  10.9 0.0 copy-start.11
  11.0 12.8 %transition.1 = (f32[4,2,4,4,32,128]{5,4,3,2,1,0:T(8,128)}, f32[2,4,4,4,16,128]{5,4,3,2,1,0:T(8,128)}, f32[4,4,4,32,128]{4,3,2,1,0:T(8,128)}, bf16[4,4,4,32,128]{4,3,2,1,0:T(8,128)(2,1)}) custom-call(f32[4,2,4,4,32,128]{5,4,3,2,1,0:T(8,128)} %bitcast.34, s32[32,128]{1,0:T(8,128)} %bitcast.44, f32[128,512]{1,0:T(8,128)} %wg_ref.2, f32[128,512]{1,0:T(8,128)} %wu_ref.1, ...), custom_call_target="tpu_custom_call" | custom-call | tf_op jit(solution)/shard_map/transition/pallas_call | solution.py:360
  23.7 0.0 all-to-all-done.1
  23.8 7.1 %all-to-all-start = ((f32[32,64,128]{2,1,0:T(8,128)}), f32[32,64,128]{2,1,0:T(8,128)S(1)}, u32[]{:S(2)}, u32[]{:S(2)}) async-start(f32[32,64,128]{2,1,0:T(8,128)} %bitcast.39), calls=%async_computation | async-start | bytes 2097152 | tf_op jit(solution)/shard_map/all_to_all | solution.py:392
  30.9 3.7 %collective-permute-start.8 = (f32[128,128]{1,0:T(8,128)S(1)}, f32[128,128]{1,0:T(8,128)S(1)}, u32[]{:S(2)}, u32[]{:S(2)}) collective-permute-start(f32[128,128]{1,0:T(8,128)S(1)} %constant_dynamic-slice_fusion), channel_id=1, source_target_pairs={{0,0},{1,1},{2,2},{3,3},{4,32},{5,33},{6,34},{7,35},{8,64},{9,65},... | collective-permute-start | bytes 196616 | tf_op jit(solution)/shard_map/ppermute | solution.py:398
  34.6 0.7 copy.17.wb_ref
  35.3 4.6 %bias.1.bias_ref = f32[128,512]{1,0:T(8,128)} custom-call(f32[4096,128]{1,0:T(8,128)} %bitcast.31, f32[128,16]{1,0:T(8,128)} %copy.17.wb_ref), custom_call_target="tpu_custom_call" | custom-call | tf_op jit(solution)/shard_map/bias/pallas_call | solution.py:400
  40.0 0.0 collective-permute-done.8.xc_ref
  40.0 0.6 copy-done.10
  40.6 4.3 %attention.1 = (f32[512,128]{1,0:T(8,128)}, f32[64,128]{1,0:T(8,128)}, f32[32,128]{1,0:T(8,128)}, f32[4,384]{1,0:T(4,128)}) custom-call(f32[512,128]{1,0:T(8,128)} %bitcast.36, f32[128,128]{1,0:T(8,128)} %copy-done.10, f32[128,512]{1,0:T(8,128)} %bias.1.bias_ref, f32[384,384]{1,0:T(8,128)} %wq_ref.1, f32[384,384]{1,0:T(8,128)} %wk_ref.1, f32[384,384]{1,0:T(8,128)} %wv_ref.1, ...), custom_call_target="tpu_custom_call" | custom-call | tf_op jit(solution)/shard_map/attention/pallas_call | solution.py:410
  44.9 5.3 %all-to-all-done = f32[32,64,128]{2,1,0:T(8,128)S(1)} async-done(((f32[32,64,128]{2,1,0:T(8,128)}), f32[32,64,128]{2,1,0:T(8,128)S(1)}, u32[]{:S(2)}, u32[]{:S(2)}) %all-to-all-start) | async-done | bytes 1048608 | tf_op jit(solution)/shard_map/all_to_all | solution.py:392
  50.2 8.3 %all-to-all-start.2 = ((f32[32,16,128]{2,1,0:T(8,128)}), f32[32,16,128]{2,1,0:T(8,128)S(1)}, u32[]{:S(2)}, u32[]{:S(2)}) async-start(f32[32,16,128]{2,1,0:T(8,128)} %bitcast.41), calls=%async_computation.2 | async-start | bytes 524288 | tf_op jit(solution)/shard_map/all_to_all | solution.py:429
  58.6 0.1 dynamic-slice_bitcast_fusion
  58.7 6.0 %collective-permute-start.7 = (f32[4,64,128]{2,1,0:T(8,128)S(1)}, f32[4,64,128]{2,1,0:T(8,128)S(1)}, u32[]{:S(2)}, u32[]{:S(2)}) collective-permute-start(f32[4,64,128]{2,1,0:T(8,128)S(1)} %get-tuple-element.22), channel_id=1, source_target_pairs={{0,56},{1,57},{2,58},{3,59},{4,24},{5,25},{6,26},{7,27},{8,120},{9... | collective-permute-start | bytes 393224 | tf_op jit(solution)/shard_map/ppermute | solution.py:426
  64.6 0.7 collective-permute-start.6
  65.3 3.5 %collective-permute-start.5 = (f32[4,64,128]{2,1,0:T(8,128)S(1)}, f32[4,64,128]{2,1,0:T(8,128)S(1)}, u32[]{:S(2)}, u32[]{:S(2)}) collective-permute-start(f32[4,64,128]{2,1,0:T(8,128)S(1)} %get-tuple-element.24), channel_id=1, source_target_pairs={{0,48},{1,49},{2,50},{3,51},{4,16},{5,17},{6,18},{7,19},{8,112},{9... | collective-permute-start | bytes 393224 | tf_op jit(solution)/shard_map/ppermute | solution.py:426
  68.8 2.7 %collective-permute-start.4 = (f32[4,64,128]{2,1,0:T(8,128)S(1)}, f32[4,64,128]{2,1,0:T(8,128)S(1)}, u32[]{:S(2)}, u32[]{:S(2)}) collective-permute-start(f32[4,64,128]{2,1,0:T(8,128)S(1)} %get-tuple-element.25), channel_id=1, source_target_pairs={{0,16},{1,17},{2,18},{3,19},{4,48},{5,49},{6,50},{7,51},{8,80},{9,... | collective-permute-start | bytes 393224 | tf_op jit(solution)/shard_map/ppermute | solution.py:426
  71.5 3.7 %collective-permute-start.3 = (f32[4,64,128]{2,1,0:T(8,128)S(1)}, f32[4,64,128]{2,1,0:T(8,128)S(1)}, u32[]{:S(2)}, u32[]{:S(2)}) collective-permute-start(f32[4,64,128]{2,1,0:T(8,128)S(1)} %get-tuple-element.26), channel_id=1, source_target_pairs={{0,40},{1,41},{2,42},{3,43},{4,8},{5,9},{6,10},{7,11},{8,104},{9,1... | collective-permute-start | bytes 393224 | tf_op jit(solution)/shard_map/ppermute | solution.py:426
  75.2 4.1 %collective-permute-done.7.refs_7_ = f32[4,64,128]{2,1,0:T(8,128)S(1)} collective-permute-done((f32[4,64,128]{2,1,0:T(8,128)S(1)}, f32[4,64,128]{2,1,0:T(8,128)S(1)}, u32[]{:S(2)}, u32[]{:S(2)}) %collective-permute-start.7) | collective-permute-done | bytes 131104 | tf_op jit(solution)/shard_map/ppermute | solution.py:426
  79.4 0.0 collective-permute-start.2
  79.4 3.7 %collective-permute-done.6.refs_6_ = f32[4,64,128]{2,1,0:T(8,128)S(1)} collective-permute-done((f32[4,64,128]{2,1,0:T(8,128)S(1)}, f32[4,64,128]{2,1,0:T(8,128)S(1)}, u32[]{:S(2)}, u32[]{:S(2)}) %collective-permute-start.6) | collective-permute-done | bytes 131104 | tf_op jit(solution)/shard_map/ppermute | solution.py:426
  83.1 4.3 %collective-permute-start.1 = (f32[4,64,128]{2,1,0:T(8,128)S(1)}, f32[4,64,128]{2,1,0:T(8,128)S(1)}, u32[]{:S(2)}, u32[]{:S(2)}) collective-permute-start(f32[4,64,128]{2,1,0:T(8,128)S(1)} %get-tuple-element.28), channel_id=1, source_target_pairs={{0,32},{1,33},{2,34},{3,35},{4,0},{5,1},{6,2},{7,3},{8,96},{9,97},... | collective-permute-start | bytes 393224 | tf_op jit(solution)/shard_map/ppermute | solution.py:426
  87.3 6.1 %collective-permute-done.5.refs_5_ = f32[4,64,128]{2,1,0:T(8,128)S(1)} collective-permute-done((f32[4,64,128]{2,1,0:T(8,128)S(1)}, f32[4,64,128]{2,1,0:T(8,128)S(1)}, u32[]{:S(2)}, u32[]{:S(2)}) %collective-permute-start.5) | collective-permute-done | bytes 131104 | tf_op jit(solution)/shard_map/ppermute | solution.py:426
  93.5 1.9 %collective-permute-start = (f32[4,64,128]{2,1,0:T(8,128)S(1)}, f32[4,64,128]{2,1,0:T(8,128)S(1)}, u32[]{:S(2)}, u32[]{:S(2)}) collective-permute-start(f32[4,64,128]{2,1,0:T(8,128)S(1)} %get-tuple-element.29), channel_id=1, source_target_pairs={{0,0},{1,1},{2,2},{3,3},{4,32},{5,33},{6,34},{7,35},{8,64},{9,65},... | collective-permute-start | bytes 393224 | tf_op jit(solution)/shard_map/ppermute | solution.py:426
  95.4 0.0 collective-permute-done.4.refs_4_
  95.5 0.0 collective-permute-done.3.refs_3_
  95.5 0.0 collective-permute-done.1.refs_1_
  95.5 12.8 %collective-permute-done.refs_0_ = f32[4,64,128]{2,1,0:T(8,128)S(1)} collective-permute-done((f32[4,64,128]{2,1,0:T(8,128)S(1)}, f32[4,64,128]{2,1,0:T(8,128)S(1)}, u32[]{:S(2)}, u32[]{:S(2)}) %collective-permute-start) | collective-permute-done | bytes 131104 | tf_op jit(solution)/shard_map/ppermute | solution.py:426
  108.4 0.6 copy-done.9
  108.9 6.6 %gradient.1 = (f32[4,2,16,32,128]{4,3,2,1,0:T(8,128)}, f32[4,384]{1,0:T(4,128)}) custom-call(s32[1]{0:T(128)} %bitcast.place_ref, f32[4,64,128]{2,1,0:T(8,128)} %copy-done.9, f32[4,64,128]{2,1,0:T(8,128)} %copy-done.8, f32[4,64,128]{2,1,0:T(8,128)} %copy-done.7, f32[4,64,128]{2,1,0:T(8,128)} %copy-done.6, f32[4,64,128]{2,1,0:T(8,128)} %copy-done.5, ...), custom_call_target="tpu_custom_call" | custom-call | tf_op jit(solution)/shard_map/gradient/pallas_call | solution.py:432
  (24 shorter events, 0.1 us)
Async XLA Ops:
  2.1 21.6 %all-to-all-start.1 = ((f32[32,16,128]{2,1,0:T(8,128)}), f32[32,16,128]{2,1,0:T(8,128)S(1)}, u32[]{:S(2)}, u32[]{:S(2)}) async-start(f32[32,16,128]{2,1,0:T(8,128)} %tokens.1), calls=%async_computation.1 | async-start | bytes 524288 | tf_op jit(solution)/shard_map/all_to_all | solution.py:357
  10.9 23.6 %copy-start.11 = (f32[128,16]{0,1:T(8,128)S(1)}, f32[128,16]{0,1:T(8,128)}, u32[]{:S(2)}) copy-start(f32[128,16]{0,1:T(8,128)} %param.22) | copy-start | bytes 24580
  23.7 16.2 %copy-start = (f32[32,16,128]{2,1,0:T(8,128)}, f32[32,16,128]{2,1,0:T(8,128)S(1)}, u32[]{:S(2)}) copy-start(f32[32,16,128]{2,1,0:T(8,128)S(1)} %all-to-all-done.1) | copy-start | bytes 786436
  23.8 26.4 %all-to-all-start = ((f32[32,64,128]{2,1,0:T(8,128)}), f32[32,64,128]{2,1,0:T(8,128)S(1)}, u32[]{:S(2)}, u32[]{:S(2)}) async-start(f32[32,64,128]{2,1,0:T(8,128)} %bitcast.39), calls=%async_computation | async-start | bytes 2097152 | tf_op jit(solution)/shard_map/all_to_all | solution.py:392
  30.9 9.1 %collective-permute-start.8 = (f32[128,128]{1,0:T(8,128)S(1)}, f32[128,128]{1,0:T(8,128)S(1)}, u32[]{:S(2)}, u32[]{:S(2)}) collective-permute-start(f32[128,128]{1,0:T(8,128)S(1)} %constant_dynamic-slice_fusion), channel_id=1, source_target_pairs={{0,0},{1,1},{2,2},{3,3},{4,32},{5,33},{6,34},{7,35},{8,64},{9,65},... | collective-permute-start | bytes 196616 | tf_op jit(solution)/shard_map/ppermute | solution.py:398
  40.0 0.6 copy-start.10
  50.2 45.2 %all-to-all-start.2 = ((f32[32,16,128]{2,1,0:T(8,128)}), f32[32,16,128]{2,1,0:T(8,128)S(1)}, u32[]{:S(2)}, u32[]{:S(2)}) async-start(f32[32,16,128]{2,1,0:T(8,128)} %bitcast.41), calls=%async_computation.2 | async-start | bytes 524288 | tf_op jit(solution)/shard_map/all_to_all | solution.py:429
  58.7 20.7 %collective-permute-start.7 = (f32[4,64,128]{2,1,0:T(8,128)S(1)}, f32[4,64,128]{2,1,0:T(8,128)S(1)}, u32[]{:S(2)}, u32[]{:S(2)}) collective-permute-start(f32[4,64,128]{2,1,0:T(8,128)S(1)} %get-tuple-element.22), channel_id=1, source_target_pairs={{0,56},{1,57},{2,58},{3,59},{4,24},{5,25},{6,26},{7,27},{8,120},{9... | collective-permute-start | bytes 393224 | tf_op jit(solution)/shard_map/ppermute | solution.py:426
  64.6 18.4 %collective-permute-start.6 = (f32[4,64,128]{2,1,0:T(8,128)S(1)}, f32[4,64,128]{2,1,0:T(8,128)S(1)}, u32[]{:S(2)}, u32[]{:S(2)}) collective-permute-start(f32[4,64,128]{2,1,0:T(8,128)S(1)} %get-tuple-element.23), channel_id=1, source_target_pairs={{0,24},{1,25},{2,26},{3,27},{4,56},{5,57},{6,58},{7,59},{8,88},{9,... | collective-permute-start | bytes 393224 | tf_op jit(solution)/shard_map/ppermute | solution.py:426
  65.3 28.2 %collective-permute-start.5 = (f32[4,64,128]{2,1,0:T(8,128)S(1)}, f32[4,64,128]{2,1,0:T(8,128)S(1)}, u32[]{:S(2)}, u32[]{:S(2)}) collective-permute-start(f32[4,64,128]{2,1,0:T(8,128)S(1)} %get-tuple-element.24), channel_id=1, source_target_pairs={{0,48},{1,49},{2,50},{3,51},{4,16},{5,17},{6,18},{7,19},{8,112},{9... | collective-permute-start | bytes 393224 | tf_op jit(solution)/shard_map/ppermute | solution.py:426
  68.8 26.6 %collective-permute-start.4 = (f32[4,64,128]{2,1,0:T(8,128)S(1)}, f32[4,64,128]{2,1,0:T(8,128)S(1)}, u32[]{:S(2)}, u32[]{:S(2)}) collective-permute-start(f32[4,64,128]{2,1,0:T(8,128)S(1)} %get-tuple-element.25), channel_id=1, source_target_pairs={{0,16},{1,17},{2,18},{3,19},{4,48},{5,49},{6,50},{7,51},{8,80},{9,... | collective-permute-start | bytes 393224 | tf_op jit(solution)/shard_map/ppermute | solution.py:426
  71.5 23.9 %collective-permute-start.3 = (f32[4,64,128]{2,1,0:T(8,128)S(1)}, f32[4,64,128]{2,1,0:T(8,128)S(1)}, u32[]{:S(2)}, u32[]{:S(2)}) collective-permute-start(f32[4,64,128]{2,1,0:T(8,128)S(1)} %get-tuple-element.26), channel_id=1, source_target_pairs={{0,40},{1,41},{2,42},{3,43},{4,8},{5,9},{6,10},{7,11},{8,104},{9,1... | collective-permute-start | bytes 393224 | tf_op jit(solution)/shard_map/ppermute | solution.py:426
  79.4 28.9 %copy-start.2 = (f32[4,64,128]{2,1,0:T(8,128)}, f32[4,64,128]{2,1,0:T(8,128)S(1)}, u32[]{:S(2)}) copy-start(f32[4,64,128]{2,1,0:T(8,128)S(1)} %collective-permute-done.7.refs_7_) | copy-start | bytes 393220
  79.4 16.1 %collective-permute-start.2 = (f32[4,64,128]{2,1,0:T(8,128)S(1)}, f32[4,64,128]{2,1,0:T(8,128)S(1)}, u32[]{:S(2)}, u32[]{:S(2)}) collective-permute-start(f32[4,64,128]{2,1,0:T(8,128)S(1)} %get-tuple-element.27), channel_id=1, source_target_pairs={{0,8},{1,9},{2,10},{3,11},{4,40},{5,41},{6,42},{7,43},{8,72},{9,73... | collective-permute-start | bytes 393224 | tf_op jit(solution)/shard_map/ppermute | solution.py:426
  83.1 25.2 %copy-start.3 = (f32[4,64,128]{2,1,0:T(8,128)}, f32[4,64,128]{2,1,0:T(8,128)S(1)}, u32[]{:S(2)}) copy-start(f32[4,64,128]{2,1,0:T(8,128)S(1)} %collective-permute-done.6.refs_6_) | copy-start | bytes 393220
  83.1 12.4 %collective-permute-start.1 = (f32[4,64,128]{2,1,0:T(8,128)S(1)}, f32[4,64,128]{2,1,0:T(8,128)S(1)}, u32[]{:S(2)}, u32[]{:S(2)}) collective-permute-start(f32[4,64,128]{2,1,0:T(8,128)S(1)} %get-tuple-element.28), channel_id=1, source_target_pairs={{0,32},{1,33},{2,34},{3,35},{4,0},{5,1},{6,2},{7,3},{8,96},{9,97},... | collective-permute-start | bytes 393224 | tf_op jit(solution)/shard_map/ppermute | solution.py:426
  93.5 14.8 %copy-start.4 = (f32[4,64,128]{2,1,0:T(8,128)}, f32[4,64,128]{2,1,0:T(8,128)S(1)}, u32[]{:S(2)}) copy-start(f32[4,64,128]{2,1,0:T(8,128)S(1)} %collective-permute-done.5.refs_5_) | copy-start | bytes 393220
  93.5 14.8 %collective-permute-start = (f32[4,64,128]{2,1,0:T(8,128)S(1)}, f32[4,64,128]{2,1,0:T(8,128)S(1)}, u32[]{:S(2)}, u32[]{:S(2)}) collective-permute-start(f32[4,64,128]{2,1,0:T(8,128)S(1)} %get-tuple-element.29), channel_id=1, source_target_pairs={{0,0},{1,1},{2,2},{3,3},{4,32},{5,33},{6,34},{7,35},{8,64},{9,65},... | collective-permute-start | bytes 393224 | tf_op jit(solution)/shard_map/ppermute | solution.py:426
  95.4 12.9 %copy-start.1 = (f32[32,16,128]{2,1,0:T(8,128)}, f32[32,16,128]{2,1,0:T(8,128)S(1)}, u32[]{:S(2)}) copy-start(f32[32,16,128]{2,1,0:T(8,128)S(1)} %all-to-all-done.2) | copy-start | bytes 786436
  95.4 12.9 %copy-start.5 = (f32[4,64,128]{2,1,0:T(8,128)}, f32[4,64,128]{2,1,0:T(8,128)S(1)}, u32[]{:S(2)}) copy-start(f32[4,64,128]{2,1,0:T(8,128)S(1)} %collective-permute-done.4.refs_4_) | copy-start | bytes 393220
  95.5 12.9 %copy-start.6 = (f32[4,64,128]{2,1,0:T(8,128)}, f32[4,64,128]{2,1,0:T(8,128)S(1)}, u32[]{:S(2)}) copy-start(f32[4,64,128]{2,1,0:T(8,128)S(1)} %collective-permute-done.3.refs_3_) | copy-start | bytes 393220
  95.5 12.9 %copy-start.7 = (f32[4,64,128]{2,1,0:T(8,128)}, f32[4,64,128]{2,1,0:T(8,128)S(1)}, u32[]{:S(2)}) copy-start(f32[4,64,128]{2,1,0:T(8,128)S(1)} %collective-permute-done.2.refs_2_) | copy-start | bytes 393220
  95.5 12.8 %copy-start.8 = (f32[4,64,128]{2,1,0:T(8,128)}, f32[4,64,128]{2,1,0:T(8,128)S(1)}, u32[]{:S(2)}) copy-start(f32[4,64,128]{2,1,0:T(8,128)S(1)} %collective-permute-done.1.refs_1_) | copy-start | bytes 393220
  108.3 0.6 copy-start.9

commit v2 on v1

--- a/solution.py
+++ b/solution.py
@@ -151,7 +151,7 @@
 def bias_kernel(mid_ref, wb_ref, bias_ref, w3_ref, n_ref):
     @pl.when(pl.program_id(0) == 0)
     def _():
-        w = jnp.concatenate([wb_ref[...]] * 8, axis=1)
+        w = jnp.concatenate([wb_ref[...]] * 8, axis=0).T
         lane = lanes_of((128, 128))
         for k in range(8):
             hi, lo = halves(jnp.where(lane // 16 == k, w, 0.0))
@@ -234,7 +234,7 @@
     msg_ref[pl.ds(3, 128, stride=4), :] = tail
 
 
-def merge_tokens(msg_ref, single_ref, gate_ref, wo_ref, out_ref):
+def merge_kernel(msg_ref, single_ref, gate_ref, wo_ref, out_ref):
     lane = lanes_of((32, 128))
     accs, factors, totals = [], [], []
     for t in range(4):
@@ -261,9 +261,8 @@
 
 def gradient_kernel(place_ref, *refs):
     parts = refs[:8]
-    own_ref, hits_ref, mid_ref, rowpad_ref, colpad_ref, wdt_ref = refs[8:14]
-    msg_ref, single_ref, gate_ref, wo_ref, out_ref, single_out_ref = refs[14:20]
-    f_ref, w_ref, ones_ref, pick_ref, d_ref = refs[20:]
+    own_ref, hits_ref, mid_ref, rowpad_ref, colpad_ref, wdt_ref, out_ref = refs[8:15]
+    f_ref, w_ref, ones_ref, pick_ref, d_ref = refs[15:]
 
     @pl.when(pl.program_id(0) == 0)
     def _():
@@ -303,10 +302,6 @@
     change = mm(d_ref[...], w_ref[0]) + mm(d_ref[...], w_ref[1])
     for k in range(2):
         out_ref[0, k] = mid_ref[0, k] + change[:, k * 128 : (k + 1) * 128].reshape(16, 32, 128)
-
-    @pl.when(pl.program_id(0) == 3)
-    def _():
-        merge_tokens(msg_ref, single_ref, gate_ref, wo_ref, single_out_ref)
 
 
 def tokens_kernel(single_ref, pad_ref, out_ref):
@@ -391,21 +386,24 @@
 
     spread = lax.all_to_all(
         proj.reshape(32, 64, 128), PLANE, split_axis=0, concat_axis=0, tiled=True
-    ).reshape(8, 4, 64, 128)
+    )
+    spread = spread.reshape(8, 4, 64, 128)
 
     quarter = lax.dynamic_slice_in_dim(rows_tok, (at["yl"] * 2 + at["core"]) * 128, 128, 0)
-    perm = [(flat_index(c), flat_index((c[2], c[3], c[0], c[1], c[4], c[5]))) for c in coords]
+    perm = [
+        (flat_index(c), flat_index((c[2], c[3] ^ c[1], c[0], c[1], c[4], c[5]))) for c in coords
+    ]
     cols_tok = lax.ppermute(quarter, ALL, perm)
 
     bias = pl.pallas_call(
         bias_kernel,
         grid=(2,),
-        in_specs=[pl.BlockSpec((2048, 128), lambda m: (m, 0)), full((128, 16))],
+        in_specs=[pl.BlockSpec((2048, 128), lambda m: (m, 0)), full((16, 128))],
         out_specs=pl.BlockSpec((64, 512), lambda m: (m, 0)),
         out_shape=struct(128, 512),
         scratch_shapes=[pltpu.VMEM((8, 256, 256), BF16), pltpu.VMEM((2048, 128), F32)],
         name="bias",
-    )(mid.reshape(4096, 128), w_bias)
+    )(mid.reshape(4096, 128), w_bias.T)
 
     msg, rowpad, colpad, gate = pl.pallas_call(
         attention_kernel,
@@ -428,8 +426,11 @@
 
     merged = lax.all_to_all(msg.reshape(32, 16, 128), COL, split_axis=0, concat_axis=0, tiled=True)
     merged = merged.reshape(512, 128)
+    single_out = pl.pallas_call(merge_kernel, out_shape=struct(4, 384), name="merge")(
+        merged, single, gate, w_attn_out
+    )
     grouped = pl.BlockSpec((1, 2, 16, 32, 128), lambda m, _: (m, 0, 0, 0, 0))
-    pair_out, single_out = pl.pallas_call(
+    pair_out = pl.pallas_call(
         gradient_kernel,
         grid_spec=pltpu.PrefetchScalarGridSpec(
             num_scalar_prefetch=1,
@@ -442,12 +443,8 @@
                 pl.BlockSpec((16, 128), lambda m, _: (m, 0)),
                 full((32, 128)),
                 full((64, 128)),
-                full((512, 128)),
-                full((4, 384)),
-                full((4, 384)),
-                full((384, 384)),
             ],
-            out_specs=[grouped, full((4, 384))],
+            out_specs=grouped,
             scratch_shapes=[
                 pltpu.VMEM((512, 128), F32),
                 pltpu.VMEM((2, 256, 256), BF16),
@@ -456,7 +453,7 @@
                 pltpu.VMEM((512, 256), BF16),
             ],
         ),
-        out_shape=[struct(4, 2, 16, 32, 128), struct(4, 384)],
+        out_shape=struct(4, 2, 16, 32, 128),
         name="gradient",
     )(
         place,
@@ -467,10 +464,6 @@
         rowpad,
         colpad,
         wdt,
-        merged,
-        single,
-        gate,
-        w_attn_out,
     )
     pair_out = pair_out.reshape(128, 32, 128)
     return (pair_out, single_out)

time: 116 us -> 113 us (0.974)
  the two profiles are of different devices: /device:TPU:32 before, /device:TPU:38 now
where the time goes in v2:
time: 113 us; the launch traced here: 112 us
  starting transfers between devices  68.3 us (60%)
  Pallas kernels  31.1 us (28%)
  waiting for transfers between devices  9.91 us (9%)
  local copies, waits for them, and re-layouts  2.06 us (2%)
    ppermute x8, starting transfers between devices, per_device(): parts.append(lax.ppermute(piece, ALL, perm))  39.2 us
    pallas_call x1, Pallas kernels, per_device(): pl.pallas_call(transition_kernel, grid=(4,), in_specs=[pl.BlockSpec((4, 2...  12.8 us
    all_to_all x1, starting transfers between devices, per_device(): rows_tok = lax.all_to_all(tok, COL, split_axis=0, concat_axis=0, tiled=True)  8.79 us
    ppermute x8, waiting for transfers between devices, per_device(): parts.append(lax.ppermute(piece, ALL, perm))  8.11 us
    all_to_all x1, starting transfers between devices, per_device(): lax.all_to_all(msg.reshape(32, 16, 128), COL, split_axis=0, concat_axis=0...  7.77 us
    all_to_all x1, starting transfers between devices, per_device(): lax.all_to_all(proj.reshape(32, 64, 128), PLANE, split_axis=0, concat_axi...  7.4 us
    pallas_call x1, Pallas kernels, per_device(): pl.pallas_call(gradient_kernel, grid_spec=pltpu.PrefetchScalarGridSpec(nu...  5.49 us
    ppermute x1, starting transfers between devices, per_device(): cols_tok = lax.ppermute(quarter, ALL, perm)  5.2 us
  transfers between devices with their start and end apart: 12, of which 3 were waited for; matrix products, arithmetic and copies ran while one was open for 0% of the time, Pallas kernels for 21%

profile of v2, /device:TPU:38, one launch (start us, length us, event | category | flops | bytes accessed | tf_op | source)
XLA Modules:
  0.0 112.3 jit_solution(14121879338892082817)
XLA Ops:
  0.6 1.5 %tokens.1 = f32[32,16,128]{2,1,0:T(8,128)} custom-call(f32[4,384]{1,0:T(4,128)} %single_ref.5, s32[4]{0:T(128)} %pad_ref.1), custom_call_target="tpu_custom_call" | custom-call | tf_op jit(solution)/shard_map/tokens/pallas_call | solution.py:346
  2.1 8.8 %all-to-all-start.1 = ((f32[32,16,128]{2,1,0:T(8,128)}), f32[32,16,128]{2,1,0:T(8,128)S(1)}, u32[]{:S(2)}, u32[]{:S(2)}) async-start(f32[32,16,128]{2,1,0:T(8,128)} %tokens.1), calls=%async_computation.1 | async-start | bytes 524288 | tf_op jit(solution)/shard_map/all_to_all | solution.py:352
  10.9 12.8 %transition.1 = (f32[4,2,4,4,32,128]{5,4,3,2,1,0:T(8,128)}, f32[2,4,4,4,16,128]{5,4,3,2,1,0:T(8,128)}, f32[4,4,4,32,128]{4,3,2,1,0:T(8,128)}, bf16[4,4,4,32,128]{4,3,2,1,0:T(8,128)(2,1)}) custom-call(f32[4,2,4,4,32,128]{5,4,3,2,1,0:T(8,128)} %bitcast.35, s32[32,128]{1,0:T(8,128)} %bitcast.46, f32[128,512]{1,0:T(8,128)} %wg_ref.2, f32[128,512]{1,0:T(8,128)} %wu_ref.1, ...), custom_call_target="tpu_custom_call" | custom-call | tf_op jit(solution)/shard_map/transition/pallas_call | solution.py:355
  23.7 7.4 %all-to-all-start = ((f32[32,64,128]{2,1,0:T(8,128)}), f32[32,64,128]{2,1,0:T(8,128)S(1)}, u32[]{:S(2)}, u32[]{:S(2)}) async-start(f32[32,64,128]{2,1,0:T(8,128)} %bitcast.39), calls=%async_computation | async-start | bytes 2097152 | tf_op jit(solution)/shard_map/all_to_all | solution.py:387
  31.2 5.2 %collective-permute-start.8 = (f32[128,128]{1,0:T(8,128)S(1)}, f32[128,128]{1,0:T(8,128)S(1)}, u32[]{:S(2)}, u32[]{:S(2)}) collective-permute-start(f32[128,128]{1,0:T(8,128)S(1)} %constant_dynamic-slice_fusion), channel_id=1, source_target_pairs={{0,0},{1,1},{2,2},{3,3},{4,32},{5,33},{6,34},{7,35},{8,64},{9,65},... | collective-permute-start | bytes 196616 | tf_op jit(solution)/shard_map/ppermute | solution.py:396
  36.4 4.5 %bias.1.bias_ref = f32[128,512]{1,0:T(8,128)} custom-call(f32[4096,128]{1,0:T(8,128)} %bitcast.32, f32[16,128]{1,0:T(8,128)} %bitcast.47), custom_call_target="tpu_custom_call" | custom-call | tf_op jit(solution)/shard_map/bias/pallas_call | solution.py:398
  40.9 0.0 collective-permute-done.8.xc_ref
  40.9 0.6 copy-done.10
  41.6 4.3 %attention.1 = (f32[512,128]{1,0:T(8,128)}, f32[64,128]{1,0:T(8,128)}, f32[32,128]{1,0:T(8,128)}, f32[4,384]{1,0:T(4,128)}) custom-call(f32[512,128]{1,0:T(8,128)} %bitcast.38, f32[128,128]{1,0:T(8,128)} %copy-done.10, f32[128,512]{1,0:T(8,128)} %bias.1.bias_ref, f32[384,384]{1,0:T(8,128)} %wq_ref.1, f32[384,384]{1,0:T(8,128)} %wk_ref.1, f32[384,384]{1,0:T(8,128)} %wv_ref.1, ...), custom_call_target="tpu_custom_call" | custom-call | tf_op jit(solution)/shard_map/attention/pallas_call | solution.py:408
  45.9 1.8 %all-to-all-done = f32[32,64,128]{2,1,0:T(8,128)S(1)} async-done(((f32[32,64,128]{2,1,0:T(8,128)}), f32[32,64,128]{2,1,0:T(8,128)S(1)}, u32[]{:S(2)}, u32[]{:S(2)}) %all-to-all-start) | async-done | bytes 1048608 | tf_op jit(solution)/shard_map/all_to_all | solution.py:387
  47.7 7.8 %all-to-all-start.2 = ((f32[32,16,128]{2,1,0:T(8,128)}), f32[32,16,128]{2,1,0:T(8,128)S(1)}, u32[]{:S(2)}, u32[]{:S(2)}) async-start(f32[32,16,128]{2,1,0:T(8,128)} %bitcast.43), calls=%async_computation.2 | async-start | bytes 524288 | tf_op jit(solution)/shard_map/all_to_all | solution.py:427
  55.5 0.1 dynamic-slice_bitcast_fusion
  55.6 7.3 %collective-permute-start.7 = (f32[4,64,128]{2,1,0:T(8,128)S(1)}, f32[4,64,128]{2,1,0:T(8,128)S(1)}, u32[]{:S(2)}, u32[]{:S(2)}) collective-permute-start(f32[4,64,128]{2,1,0:T(8,128)S(1)} %get-tuple-element.18), channel_id=1, source_target_pairs={{0,56},{1,57},{2,58},{3,59},{4,24},{5,25},{6,26},{7,27},{8,120},{9... | collective-permute-start | bytes 393224 | tf_op jit(solution)/shard_map/ppermute | solution.py:424
  62.9 1.1 collective-permute-start.6
  64.0 4.0 %collective-permute-start.5 = (f32[4,64,128]{2,1,0:T(8,128)S(1)}, f32[4,64,128]{2,1,0:T(8,128)S(1)}, u32[]{:S(2)}, u32[]{:S(2)}) collective-permute-start(f32[4,64,128]{2,1,0:T(8,128)S(1)} %get-tuple-element.20), channel_id=1, source_target_pairs={{0,48},{1,49},{2,50},{3,51},{4,16},{5,17},{6,18},{7,19},{8,112},{9... | collective-permute-start | bytes 393224 | tf_op jit(solution)/shard_map/ppermute | solution.py:424
  68.0 1.4 %collective-permute-start.4 = (f32[4,64,128]{2,1,0:T(8,128)S(1)}, f32[4,64,128]{2,1,0:T(8,128)S(1)}, u32[]{:S(2)}, u32[]{:S(2)}) collective-permute-start(f32[4,64,128]{2,1,0:T(8,128)S(1)} %get-tuple-element.21), channel_id=1, source_target_pairs={{0,16},{1,17},{2,18},{3,19},{4,48},{5,49},{6,50},{7,51},{8,80},{9,... | collective-permute-start | bytes 393224 | tf_op jit(solution)/shard_map/ppermute | solution.py:424
  69.4 6.6 %collective-permute-start.3 = (f32[4,64,128]{2,1,0:T(8,128)S(1)}, f32[4,64,128]{2,1,0:T(8,128)S(1)}, u32[]{:S(2)}, u32[]{:S(2)}) collective-permute-start(f32[4,64,128]{2,1,0:T(8,128)S(1)} %get-tuple-element.22), channel_id=1, source_target_pairs={{0,40},{1,41},{2,42},{3,43},{4,8},{5,9},{6,10},{7,11},{8,104},{9,1... | collective-permute-start | bytes 393224 | tf_op jit(solution)/shard_map/ppermute | solution.py:424
  76.0 0.0 collective-permute-done.7.refs_7_
  76.0 10.1 %collective-permute-start.2 = (f32[4,64,128]{2,1,0:T(8,128)S(1)}, f32[4,64,128]{2,1,0:T(8,128)S(1)}, u32[]{:S(2)}, u32[]{:S(2)}) collective-permute-start(f32[4,64,128]{2,1,0:T(8,128)S(1)} %get-tuple-element.23), channel_id=1, source_target_pairs={{0,8},{1,9},{2,10},{3,11},{4,40},{5,41},{6,42},{7,43},{8,72},{9,73... | collective-permute-start | bytes 393224 | tf_op jit(solution)/shard_map/ppermute | solution.py:424
  86.1 0.0 collective-permute-done.6.refs_6_
  86.1 2.4 %collective-permute-start.1 = (f32[4,64,128]{2,1,0:T(8,128)S(1)}, f32[4,64,128]{2,1,0:T(8,128)S(1)}, u32[]{:S(2)}, u32[]{:S(2)}) collective-permute-start(f32[4,64,128]{2,1,0:T(8,128)S(1)} %get-tuple-element.24), channel_id=1, source_target_pairs={{0,32},{1,33},{2,34},{3,35},{4,0},{5,1},{6,2},{7,3},{8,96},{9,97},... | collective-permute-start | bytes 393224 | tf_op jit(solution)/shard_map/ppermute | solution.py:424
  88.4 0.0 collective-permute-done.5.refs_5_
  88.5 6.3 %collective-permute-start = (f32[4,64,128]{2,1,0:T(8,128)S(1)}, f32[4,64,128]{2,1,0:T(8,128)S(1)}, u32[]{:S(2)}, u32[]{:S(2)}) collective-permute-start(f32[4,64,128]{2,1,0:T(8,128)S(1)} %get-tuple-element.25), channel_id=1, source_target_pairs={{0,0},{1,1},{2,2},{3,3},{4,32},{5,33},{6,34},{7,35},{8,64},{9,65},... | collective-permute-start | bytes 393224 | tf_op jit(solution)/shard_map/ppermute | solution.py:424
  94.8 0.0 copy-start.1
  94.8 0.7 copy-done.1
  95.5 2.5 %merge.1 = f32[4,384]{1,0:T(4,128)} custom-call(f32[512,128]{1,0:T(8,128)} %bitcast.40, f32[4,384]{1,0:T(4,128)} %single_ref.5, f32[4,384]{1,0:T(4,128)} %get-tuple-element.17.gate_ref, f32[384,384]{1,0:T(8,128)} %wo_ref.3), custom_call_target="tpu_custom_call" | custom-call | tf_op jit(solution)/shard_map/merge/pallas_call | solution.py:429
  98.0 0.0 collective-permute-done.4.refs_4_
  98.0 0.0 collective-permute-done.2.refs_2_
  98.0 3.7 %collective-permute-done.1.refs_1_ = f32[4,64,128]{2,1,0:T(8,128)S(1)} collective-permute-done((f32[4,64,128]{2,1,0:T(8,128)S(1)}, f32[4,64,128]{2,1,0:T(8,128)S(1)}, u32[]{:S(2)}, u32[]{:S(2)}) %collective-permute-start.1) | collective-permute-done | bytes 131104 | tf_op jit(solution)/shard_map/ppermute | solution.py:424
  101.8 4.4 %collective-permute-done.refs_0_ = f32[4,64,128]{2,1,0:T(8,128)S(1)} collective-permute-done((f32[4,64,128]{2,1,0:T(8,128)S(1)}, f32[4,64,128]{2,1,0:T(8,128)S(1)}, u32[]{:S(2)}, u32[]{:S(2)}) %collective-permute-start) | collective-permute-done | bytes 131104 | tf_op jit(solution)/shard_map/ppermute | solution.py:424
  106.2 0.6 copy-done.9
  106.8 5.5 %gradient.1 = f32[4,2,16,32,128]{4,3,2,1,0:T(8,128)} custom-call(s32[1]{0:T(128)} %bitcast.place_ref, f32[4,64,128]{2,1,0:T(8,128)} %copy-done.9, f32[4,64,128]{2,1,0:T(8,128)} %copy-done.8, f32[4,64,128]{2,1,0:T(8,128)} %copy-done.7, f32[4,64,128]{2,1,0:T(8,128)} %copy-done.6, f32[4,64,128]{2,1,0:T(8,128)} %copy-done.5, f32[4,64,128]{2,1,0:T(8,128)} %copy-done.4, ...), custom_call_target="tpu_custom_call" | custom-call | tf_op jit(solution)/shard_map/gradient/pallas_call | solution.py:433
  (22 shorter events, 0.1 us)
Async XLA Ops:
  2.1 21.6 %all-to-all-start.1 = ((f32[32,16,128]{2,1,0:T(8,128)}), f32[32,16,128]{2,1,0:T(8,128)S(1)}, u32[]{:S(2)}, u32[]{:S(2)}) async-start(f32[32,16,128]{2,1,0:T(8,128)} %tokens.1), calls=%async_computation.1 | async-start | bytes 524288 | tf_op jit(solution)/shard_map/all_to_all | solution.py:352
  23.7 17.2 %copy-start = (f32[32,16,128]{2,1,0:T(8,128)}, f32[32,16,128]{2,1,0:T(8,128)S(1)}, u32[]{:S(2)}) copy-start(f32[32,16,128]{2,1,0:T(8,128)S(1)} %all-to-all-done.1) | copy-start | bytes 786436
  23.7 23.9 %all-to-all-start = ((f32[32,64,128]{2,1,0:T(8,128)}), f32[32,64,128]{2,1,0:T(8,128)S(1)}, u32[]{:S(2)}, u32[]{:S(2)}) async-start(f32[32,64,128]{2,1,0:T(8,128)} %bitcast.39), calls=%async_computation | async-start | bytes 2097152 | tf_op jit(solution)/shard_map/all_to_all | solution.py:387
  31.2 9.8 %collective-permute-start.8 = (f32[128,128]{1,0:T(8,128)S(1)}, f32[128,128]{1,0:T(8,128)S(1)}, u32[]{:S(2)}, u32[]{:S(2)}) collective-permute-start(f32[128,128]{1,0:T(8,128)S(1)} %constant_dynamic-slice_fusion), channel_id=1, source_target_pairs={{0,0},{1,1},{2,2},{3,3},{4,32},{5,33},{6,34},{7,35},{8,64},{9,65},... | collective-permute-start | bytes 196616 | tf_op jit(solution)/shard_map/ppermute | solution.py:396
  40.9 0.6 copy-start.10
  47.7 47.1 %all-to-all-start.2 = ((f32[32,16,128]{2,1,0:T(8,128)}), f32[32,16,128]{2,1,0:T(8,128)S(1)}, u32[]{:S(2)}, u32[]{:S(2)}) async-start(f32[32,16,128]{2,1,0:T(8,128)} %bitcast.43), calls=%async_computation.2 | async-start | bytes 524288 | tf_op jit(solution)/shard_map/all_to_all | solution.py:427
  55.6 20.4 %collective-permute-start.7 = (f32[4,64,128]{2,1,0:T(8,128)S(1)}, f32[4,64,128]{2,1,0:T(8,128)S(1)}, u32[]{:S(2)}, u32[]{:S(2)}) collective-permute-start(f32[4,64,128]{2,1,0:T(8,128)S(1)} %get-tuple-element.18), channel_id=1, source_target_pairs={{0,56},{1,57},{2,58},{3,59},{4,24},{5,25},{6,26},{7,27},{8,120},{9... | collective-permute-start | bytes 393224 | tf_op jit(solution)/shard_map/ppermute | solution.py:424
  62.9 23.2 %collective-permute-start.6 = (f32[4,64,128]{2,1,0:T(8,128)S(1)}, f32[4,64,128]{2,1,0:T(8,128)S(1)}, u32[]{:S(2)}, u32[]{:S(2)}) collective-permute-start(f32[4,64,128]{2,1,0:T(8,128)S(1)} %get-tuple-element.19), channel_id=1, source_target_pairs={{0,24},{1,25},{2,26},{3,27},{4,56},{5,57},{6,58},{7,59},{8,88},{9,... | collective-permute-start | bytes 393224 | tf_op jit(solution)/shard_map/ppermute | solution.py:424
  64.0 24.5 %collective-permute-start.5 = (f32[4,64,128]{2,1,0:T(8,128)S(1)}, f32[4,64,128]{2,1,0:T(8,128)S(1)}, u32[]{:S(2)}, u32[]{:S(2)}) collective-permute-start(f32[4,64,128]{2,1,0:T(8,128)S(1)} %get-tuple-element.20), channel_id=1, source_target_pairs={{0,48},{1,49},{2,50},{3,51},{4,16},{5,17},{6,18},{7,19},{8,112},{9... | collective-permute-start | bytes 393224 | tf_op jit(solution)/shard_map/ppermute | solution.py:424
  68.0 30.0 %collective-permute-start.4 = (f32[4,64,128]{2,1,0:T(8,128)S(1)}, f32[4,64,128]{2,1,0:T(8,128)S(1)}, u32[]{:S(2)}, u32[]{:S(2)}) collective-permute-start(f32[4,64,128]{2,1,0:T(8,128)S(1)} %get-tuple-element.21), channel_id=1, source_target_pairs={{0,16},{1,17},{2,18},{3,19},{4,48},{5,49},{6,50},{7,51},{8,80},{9,... | collective-permute-start | bytes 393224 | tf_op jit(solution)/shard_map/ppermute | solution.py:424
  69.4 28.6 %collective-permute-start.3 = (f32[4,64,128]{2,1,0:T(8,128)S(1)}, f32[4,64,128]{2,1,0:T(8,128)S(1)}, u32[]{:S(2)}, u32[]{:S(2)}) collective-permute-start(f32[4,64,128]{2,1,0:T(8,128)S(1)} %get-tuple-element.22), channel_id=1, source_target_pairs={{0,40},{1,41},{2,42},{3,43},{4,8},{5,9},{6,10},{7,11},{8,104},{9,1... | collective-permute-start | bytes 393224 | tf_op jit(solution)/shard_map/ppermute | solution.py:424
  76.0 30.1 %copy-start.2 = (f32[4,64,128]{2,1,0:T(8,128)}, f32[4,64,128]{2,1,0:T(8,128)S(1)}, u32[]{:S(2)}) copy-start(f32[4,64,128]{2,1,0:T(8,128)S(1)} %collective-permute-done.7.refs_7_) | copy-start | bytes 393220
  76.0 22.0 %collective-permute-start.2 = (f32[4,64,128]{2,1,0:T(8,128)S(1)}, f32[4,64,128]{2,1,0:T(8,128)S(1)}, u32[]{:S(2)}, u32[]{:S(2)}) collective-permute-start(f32[4,64,128]{2,1,0:T(8,128)S(1)} %get-tuple-element.23), channel_id=1, source_target_pairs={{0,8},{1,9},{2,10},{3,11},{4,40},{5,41},{6,42},{7,43},{8,72},{9,73... | collective-permute-start | bytes 393224 | tf_op jit(solution)/shard_map/ppermute | solution.py:424
  86.1 20.1 %copy-start.3 = (f32[4,64,128]{2,1,0:T(8,128)}, f32[4,64,128]{2,1,0:T(8,128)S(1)}, u32[]{:S(2)}) copy-start(f32[4,64,128]{2,1,0:T(8,128)S(1)} %collective-permute-done.6.refs_6_) | copy-start | bytes 393220
  86.1 15.7 %collective-permute-start.1 = (f32[4,64,128]{2,1,0:T(8,128)S(1)}, f32[4,64,128]{2,1,0:T(8,128)S(1)}, u32[]{:S(2)}, u32[]{:S(2)}) collective-permute-start(f32[4,64,128]{2,1,0:T(8,128)S(1)} %get-tuple-element.24), channel_id=1, source_target_pairs={{0,32},{1,33},{2,34},{3,35},{4,0},{5,1},{6,2},{7,3},{8,96},{9,97},... | collective-permute-start | bytes 393224 | tf_op jit(solution)/shard_map/ppermute | solution.py:424
  88.5 17.7 %copy-start.4 = (f32[4,64,128]{2,1,0:T(8,128)}, f32[4,64,128]{2,1,0:T(8,128)S(1)}, u32[]{:S(2)}) copy-start(f32[4,64,128]{2,1,0:T(8,128)S(1)} %collective-permute-done.5.refs_5_) | copy-start | bytes 393220
  88.5 17.7 %collective-permute-start = (f32[4,64,128]{2,1,0:T(8,128)S(1)}, f32[4,64,128]{2,1,0:T(8,128)S(1)}, u32[]{:S(2)}, u32[]{:S(2)}) collective-permute-start(f32[4,64,128]{2,1,0:T(8,128)S(1)} %get-tuple-element.25), channel_id=1, source_target_pairs={{0,0},{1,1},{2,2},{3,3},{4,32},{5,33},{6,34},{7,35},{8,64},{9,65},... | collective-permute-start | bytes 393224 | tf_op jit(solution)/shard_map/ppermute | solution.py:424
  94.8 0.7 copy-start.1
  98.0 8.2 %copy-start.5 = (f32[4,64,128]{2,1,0:T(8,128)}, f32[4,64,128]{2,1,0:T(8,128)S(1)}, u32[]{:S(2)}) copy-start(f32[4,64,128]{2,1,0:T(8,128)S(1)} %collective-permute-done.4.refs_4_) | copy-start | bytes 393220
  98.0 8.2 %copy-start.6 = (f32[4,64,128]{2,1,0:T(8,128)}, f32[4,64,128]{2,1,0:T(8,128)S(1)}, u32[]{:S(2)}) copy-start(f32[4,64,128]{2,1,0:T(8,128)S(1)} %collective-permute-done.3.refs_3_) | copy-start | bytes 393220
  98.0 8.1 %copy-start.7 = (f32[4,64,128]{2,1,0:T(8,128)}, f32[4,64,128]{2,1,0:T(8,128)S(1)}, u32[]{:S(2)}) copy-start(f32[4,64,128]{2,1,0:T(8,128)S(1)} %collective-permute-done.2.refs_2_) | copy-start | bytes 393220
  101.8 4.4 %copy-start.8 = (f32[4,64,128]{2,1,0:T(8,128)}, f32[4,64,128]{2,1,0:T(8,128)S(1)}, u32[]{:S(2)}) copy-start(f32[4,64,128]{2,1,0:T(8,128)S(1)} %collective-permute-done.1.refs_1_) | copy-start | bytes 393220
  106.1 0.6 copy-start.9

commit v3 on v2

--- a/solution.py
+++ b/solution.py
@@ -281,7 +281,7 @@
 
     for p in range(8):
         place = place_ref[0] ^ p
-        f_ref[pl.ds(pl.multiple_of(place * 64, 64), 64), :] = parts[p][0]
+        f_ref[pl.ds(pl.multiple_of(place * 64, 64), 64), :] = parts[p][pl.program_id(0)]
 
     lane = lanes_of((512, 128))
     first = lane < 64
@@ -315,6 +315,10 @@
 
 def full(shape):
     return pl.BlockSpec(shape, lambda *_: (0,) * len(shape))
+
+
+def near(x):
+    return pltpu.with_memory_space_constraint(x, pltpu.VMEM)
 
 
 def struct(*shape):
@@ -407,9 +411,10 @@
 
     msg, rowpad, colpad, gate = pl.pallas_call(
         attention_kernel,
+        in_specs=[pl.BlockSpec(memory_space=pltpu.VMEM)] * 8,
         out_shape=[struct(512, 128), struct(64, 128), struct(32, 128), struct(4, 384)],
         name="attention",
-    )(rows_tok, cols_tok, bias, w_query, w_key, w_value, single, w_gating)
+    )(near(rows_tok), near(cols_tok), bias, w_query, w_key, w_value, single, w_gating)
 
     parts = []
     for n in range(8):
@@ -426,8 +431,13 @@
 
     merged = lax.all_to_all(msg.reshape(32, 16, 128), COL, split_axis=0, concat_axis=0, tiled=True)
     merged = merged.reshape(512, 128)
-    single_out = pl.pallas_call(merge_kernel, out_shape=struct(4, 384), name="merge")(
-        merged, single, gate, w_attn_out
+    single_out = pl.pallas_call(
+        merge_kernel,
+        in_specs=[pl.BlockSpec(memory_space=pltpu.VMEM)] * 4,
+        out_shape=struct(4, 384),
+        name="merge",
+    )(
+        near(merged), single, gate, w_attn_out
     )
     grouped = pl.BlockSpec((1, 2, 16, 32, 128), lambda m, _: (m, 0, 0, 0, 0))
     pair_out = pl.pallas_call(
@@ -435,7 +445,7 @@
         grid_spec=pltpu.PrefetchScalarGridSpec(
             num_scalar_prefetch=1,
             grid=(4,),
-            in_specs=[pl.BlockSpec((1, 64, 128), lambda m, _: (m, 0, 0))] * 8
+            in_specs=[pl.BlockSpec(memory_space=pltpu.VMEM)] * 8
             + [
                 pl.BlockSpec((16, 32, 128), lambda m, _: (m, 0, 0)),
                 pl.BlockSpec((16, 32, 128), lambda m, _: (m, 0, 0)),
@@ -457,7 +467,7 @@
         name="gradient",
     )(
         place,
-        *parts,
+        *(near(p) for p in parts),
         own.reshape(64, 32, 128),
         hits.reshape(64, 32, 128),
         mid.reshape(4, 2, 16, 32, 128),

time: 113 us -> 111 us (0.982)
  local copies, waits for them, and re-layouts: 2.06 us -> 0.11 us
  waiting for transfers between devices: 9.91 us -> 11.5 us
    unnamed x22 -> x0, local copies, waits for them, and re-layouts: 1.95 us -> none
  transfers between devices with their start and end apart: 12 -> 12, of which waited for: 3 -> 3; matrix products, arithmetic and copies ran while one was open for 0% -> 0% of each run, Pallas kernels for 21% -> 22%
where the time goes in v3:
time: 111 us
  starting transfers between devices  67.6 us (61%)
  Pallas kernels  30.6 us (28%)
  waiting for transfers between devices  11.5 us (10%)
    ppermute x8, starting transfers between devices, per_device(): parts.append(lax.ppermute(piece, ALL, perm))  39.1 us
    pallas_call x1, Pallas kernels, per_device(): pl.pallas_call(transition_kernel, grid=(4,), in_specs=[pl.BlockSpec((4, 2...  12.8 us
    ppermute x8, waiting for transfers between devices, per_device(): parts.append(lax.ppermute(piece, ALL, perm))  8.94 us
    all_to_all x1, starting transfers between devices, per_device(): rows_tok = lax.all_to_all(tok, COL, split_axis=0, concat_axis=0, tiled=True)  8.79 us
    all_to_all x1, starting transfers between devices, per_device(): lax.all_to_all(proj.reshape(32, 64, 128), PLANE, split_axis=0, concat_axi...  7.4 us
    all_to_all x1, starting transfers between devices, per_device(): lax.all_to_all(msg.reshape(32, 16, 128), COL, split_axis=0, concat_axis=0...  7.06 us
    ppermute x1, starting transfers between devices, per_device(): cols_tok = lax.ppermute(quarter, ALL, perm)  5.19 us
    pallas_call x1, Pallas kernels, per_device(): pl.pallas_call(gradient_kernel, grid_spec=pltpu.PrefetchScalarGridSpec(nu...  5.16 us
  transfers between devices with their start and end apart: 12, of which 3 were waited for; matrix products, arithmetic and copies ran while one was open for 0% of the time, Pallas kernels for 22%

profile of v3, /device:TPU:38, one launch (start us, length us, event | category | flops | bytes accessed | tf_op | source)
XLA Modules:
  0.0 110.5 jit_solution(16549161380603101674)
XLA Ops:
  0.6 1.5 %tokens.1 = f32[32,16,128]{2,1,0:T(8,128)} custom-call(f32[4,384]{1,0:T(4,128)} %single_ref.5, s32[4]{0:T(128)} %pad_ref.1), custom_call_target="tpu_custom_call" | custom-call | tf_op jit(solution)/shard_map/tokens/pallas_call | solution.py:350
  2.2 8.8 %all-to-all-start.1 = ((f32[32,16,128]{2,1,0:T(8,128)}), f32[32,16,128]{2,1,0:T(8,128)S(1)}, u32[]{:S(2)}, u32[]{:S(2)}) async-start(f32[32,16,128]{2,1,0:T(8,128)} %tokens.1), calls=%async_computation.1 | async-start | bytes 524288 | tf_op jit(solution)/shard_map/all_to_all | solution.py:356
  11.0 12.8 %transition.1 = (f32[4,2,4,4,32,128]{5,4,3,2,1,0:T(8,128)}, f32[2,4,4,4,16,128]{5,4,3,2,1,0:T(8,128)}, f32[4,4,4,32,128]{4,3,2,1,0:T(8,128)}, bf16[4,4,4,32,128]{4,3,2,1,0:T(8,128)(2,1)}) custom-call(f32[4,2,4,4,32,128]{5,4,3,2,1,0:T(8,128)} %bitcast.38, s32[32,128]{1,0:T(8,128)} %bitcast.46, f32[128,512]{1,0:T(8,128)} %wg_ref.2, f32[128,512]{1,0:T(8,128)} %wu_ref.1, ...), custom_call_target="tpu_custom_call" | custom-call | tf_op jit(solution)/shard_map/transition/pallas_call | solution.py:359
  23.7 0.0 all-to-all-done.1
  23.7 7.4 %all-to-all-start = ((f32[32,64,128]{2,1,0:T(8,128)}), f32[32,64,128]{2,1,0:T(8,128)S(1)}, u32[]{:S(2)}, u32[]{:S(2)}) async-start(f32[32,64,128]{2,1,0:T(8,128)} %bitcast.40), calls=%async_computation | async-start | bytes 2097152 | tf_op jit(solution)/shard_map/all_to_all | solution.py:391
  31.2 5.2 %collective-permute-start.8 = (f32[128,128]{1,0:T(8,128)S(1)}, f32[128,128]{1,0:T(8,128)S(1)}, u32[]{:S(2)}, u32[]{:S(2)}) collective-permute-start(f32[128,128]{1,0:T(8,128)S(1)} %constant_dynamic-slice_fusion), channel_id=1, source_target_pairs={{0,0},{1,1},{2,2},{3,3},{4,32},{5,33},{6,34},{7,35},{8,64},{9,65},... | collective-permute-start | bytes 196616 | tf_op jit(solution)/shard_map/ppermute | solution.py:400
  36.3 4.6 %bias.1.bias_ref = f32[128,512]{1,0:T(8,128)} custom-call(f32[4096,128]{1,0:T(8,128)} %bitcast.35, f32[16,128]{1,0:T(8,128)} %bitcast.47), custom_call_target="tpu_custom_call" | custom-call | tf_op jit(solution)/shard_map/bias/pallas_call | solution.py:402
  40.9 0.0 collective-permute-done.8.xc_ref
  40.9 4.2 %attention.1 = (f32[512,128]{1,0:T(8,128)}, f32[64,128]{1,0:T(8,128)}, f32[32,128]{1,0:T(8,128)}, f32[4,384]{1,0:T(4,128)}) custom-call(f32[512,128]{1,0:T(8,128)S(1)} %bitcast.33, f32[128,128]{1,0:T(8,128)S(1)} %collective-permute-done.8.xc_ref, f32[128,512]{1,0:T(8,128)} %bias.1.bias_ref, f32[384,384]{1,0:T(8,128)} %wq_ref.1, f32[384,384]{1,0:T(8,128)} %wk_ref.1, ...), custom_call_target="tpu_custom_call" | custom-call | tf_op jit(solution)/shard_map/attention/pallas_call | solution.py:412
  45.1 2.5 %all-to-all-done = f32[32,64,128]{2,1,0:T(8,128)S(1)} async-done(((f32[32,64,128]{2,1,0:T(8,128)}), f32[32,64,128]{2,1,0:T(8,128)S(1)}, u32[]{:S(2)}, u32[]{:S(2)}) %all-to-all-start) | async-done | bytes 1048608 | tf_op jit(solution)/shard_map/all_to_all | solution.py:391
  47.6 7.1 %all-to-all-start.2 = ((f32[32,16,128]{2,1,0:T(8,128)}), f32[32,16,128]{2,1,0:T(8,128)S(1)}, u32[]{:S(2)}, u32[]{:S(2)}) async-start(f32[32,16,128]{2,1,0:T(8,128)} %bitcast.43), calls=%async_computation.2 | async-start | bytes 524288 | tf_op jit(solution)/shard_map/all_to_all | solution.py:432
  54.8 0.1 dynamic-slice_bitcast_fusion
  54.9 7.3 %collective-permute-start.7 = (f32[4,64,128]{2,1,0:T(8,128)S(1)}, f32[4,64,128]{2,1,0:T(8,128)S(1)}, u32[]{:S(2)}, u32[]{:S(2)}) collective-permute-start(f32[4,64,128]{2,1,0:T(8,128)S(1)} %get-tuple-element.18), channel_id=1, source_target_pairs={{0,56},{1,57},{2,58},{3,59},{4,24},{5,25},{6,26},{7,27},{8,120},{9... | collective-permute-start | bytes 393224 | tf_op jit(solution)/shard_map/ppermute | solution.py:429
  62.1 1.1 %collective-permute-start.6 = (f32[4,64,128]{2,1,0:T(8,128)S(1)}, f32[4,64,128]{2,1,0:T(8,128)S(1)}, u32[]{:S(2)}, u32[]{:S(2)}) collective-permute-start(f32[4,64,128]{2,1,0:T(8,128)S(1)} %get-tuple-element.19), channel_id=1, source_target_pairs={{0,24},{1,25},{2,26},{3,27},{4,56},{5,57},{6,58},{7,59},{8,88},{9,... | collective-permute-start | bytes 393224 | tf_op jit(solution)/shard_map/ppermute | solution.py:429
  63.2 4.0 %collective-permute-start.5 = (f32[4,64,128]{2,1,0:T(8,128)S(1)}, f32[4,64,128]{2,1,0:T(8,128)S(1)}, u32[]{:S(2)}, u32[]{:S(2)}) collective-permute-start(f32[4,64,128]{2,1,0:T(8,128)S(1)} %get-tuple-element.20), channel_id=1, source_target_pairs={{0,48},{1,49},{2,50},{3,51},{4,16},{5,17},{6,18},{7,19},{8,112},{9... | collective-permute-start | bytes 393224 | tf_op jit(solution)/shard_map/ppermute | solution.py:429
  67.2 1.4 %collective-permute-start.4 = (f32[4,64,128]{2,1,0:T(8,128)S(1)}, f32[4,64,128]{2,1,0:T(8,128)S(1)}, u32[]{:S(2)}, u32[]{:S(2)}) collective-permute-start(f32[4,64,128]{2,1,0:T(8,128)S(1)} %get-tuple-element.21), channel_id=1, source_target_pairs={{0,16},{1,17},{2,18},{3,19},{4,48},{5,49},{6,50},{7,51},{8,80},{9,... | collective-permute-start | bytes 393224 | tf_op jit(solution)/shard_map/ppermute | solution.py:429
  68.6 6.6 %collective-permute-start.3 = (f32[4,64,128]{2,1,0:T(8,128)S(1)}, f32[4,64,128]{2,1,0:T(8,128)S(1)}, u32[]{:S(2)}, u32[]{:S(2)}) collective-permute-start(f32[4,64,128]{2,1,0:T(8,128)S(1)} %get-tuple-element.22), channel_id=1, source_target_pairs={{0,40},{1,41},{2,42},{3,43},{4,8},{5,9},{6,10},{7,11},{8,104},{9,1... | collective-permute-start | bytes 393224 | tf_op jit(solution)/shard_map/ppermute | solution.py:429
  75.3 0.0 collective-permute-done.7.refs_7_
  75.3 10.2 %collective-permute-start.2 = (f32[4,64,128]{2,1,0:T(8,128)S(1)}, f32[4,64,128]{2,1,0:T(8,128)S(1)}, u32[]{:S(2)}, u32[]{:S(2)}) collective-permute-start(f32[4,64,128]{2,1,0:T(8,128)S(1)} %get-tuple-element.23), channel_id=1, source_target_pairs={{0,8},{1,9},{2,10},{3,11},{4,40},{5,41},{6,42},{7,43},{8,72},{9,73... | collective-permute-start | bytes 393224 | tf_op jit(solution)/shard_map/ppermute | solution.py:429
  85.5 0.0 collective-permute-done.6.refs_6_
  85.5 2.2 %collective-permute-start.1 = (f32[4,64,128]{2,1,0:T(8,128)S(1)}, f32[4,64,128]{2,1,0:T(8,128)S(1)}, u32[]{:S(2)}, u32[]{:S(2)}) collective-permute-start(f32[4,64,128]{2,1,0:T(8,128)S(1)} %get-tuple-element.24), channel_id=1, source_target_pairs={{0,32},{1,33},{2,34},{3,35},{4,0},{5,1},{6,2},{7,3},{8,96},{9,97},... | collective-permute-start | bytes 393224 | tf_op jit(solution)/shard_map/ppermute | solution.py:429
  87.7 0.0 collective-permute-done.5.refs_5_
  87.7 6.3 %collective-permute-start = (f32[4,64,128]{2,1,0:T(8,128)S(1)}, f32[4,64,128]{2,1,0:T(8,128)S(1)}, u32[]{:S(2)}, u32[]{:S(2)}) collective-permute-start(f32[4,64,128]{2,1,0:T(8,128)S(1)} %get-tuple-element.25), channel_id=1, source_target_pairs={{0,0},{1,1},{2,2},{3,3},{4,32},{5,33},{6,34},{7,35},{8,64},{9,65},... | collective-permute-start | bytes 393224 | tf_op jit(solution)/shard_map/ppermute | solution.py:429
  94.0 0.0 all-to-all-done.2
  94.0 2.4 %merge.1 = f32[4,384]{1,0:T(4,128)} custom-call(f32[512,128]{1,0:T(8,128)S(1)} %bitcast.34, f32[4,384]{1,0:T(4,128)} %single_ref.5, f32[4,384]{1,0:T(4,128)} %get-tuple-element.17.gate_ref, f32[384,384]{1,0:T(8,128)} %wo_ref.3), custom_call_target="tpu_custom_call" | custom-call | tf_op jit(solution)/shard_map/merge/pallas_call | solution.py:434
  96.4 0.0 collective-permute-done.4.refs_4_
  96.4 0.0 collective-permute-done.3.refs_3_
  96.4 0.0 collective-permute-done.2.refs_2_
  96.4 4.4 %collective-permute-done.1.refs_1_ = f32[4,64,128]{2,1,0:T(8,128)S(1)} collective-permute-done((f32[4,64,128]{2,1,0:T(8,128)S(1)}, f32[4,64,128]{2,1,0:T(8,128)S(1)}, u32[]{:S(2)}, u32[]{:S(2)}) %collective-permute-start.1) | collective-permute-done | bytes 131104 | tf_op jit(solution)/shard_map/ppermute | solution.py:429
  100.9 4.5 %collective-permute-done.refs_0_ = f32[4,64,128]{2,1,0:T(8,128)S(1)} collective-permute-done((f32[4,64,128]{2,1,0:T(8,128)S(1)}, f32[4,64,128]{2,1,0:T(8,128)S(1)}, u32[]{:S(2)}, u32[]{:S(2)}) %collective-permute-start) | collective-permute-done | bytes 131104 | tf_op jit(solution)/shard_map/ppermute | solution.py:429
  105.4 5.2 %gradient.1 = f32[4,2,16,32,128]{4,3,2,1,0:T(8,128)} custom-call(s32[1]{0:T(128)} %bitcast.place_ref, f32[4,64,128]{2,1,0:T(8,128)S(1)} %collective-permute-done.refs_0_, f32[4,64,128]{2,1,0:T(8,128)S(1)} %collective-permute-done.1.refs_1_, f32[4,64,128]{2,1,0:T(8,128)S(1)} %collective-permute-done.2.refs_2_, ...), custom_call_target="tpu_custom_call" | custom-call | tf_op jit(solution)/shard_map/gradient/pallas_call | solution.py:443
  (1 shorter events, 0.0 us)
Async XLA Ops:
  2.2 21.6 %all-to-all-start.1 = ((f32[32,16,128]{2,1,0:T(8,128)}), f32[32,16,128]{2,1,0:T(8,128)S(1)}, u32[]{:S(2)}, u32[]{:S(2)}) async-start(f32[32,16,128]{2,1,0:T(8,128)} %tokens.1), calls=%async_computation.1 | async-start | bytes 524288 | tf_op jit(solution)/shard_map/all_to_all | solution.py:356
  23.7 23.9 %all-to-all-start = ((f32[32,64,128]{2,1,0:T(8,128)}), f32[32,64,128]{2,1,0:T(8,128)S(1)}, u32[]{:S(2)}, u32[]{:S(2)}) async-start(f32[32,64,128]{2,1,0:T(8,128)} %bitcast.40), calls=%async_computation | async-start | bytes 2097152 | tf_op jit(solution)/shard_map/all_to_all | solution.py:391
  31.2 9.7 %collective-permute-start.8 = (f32[128,128]{1,0:T(8,128)S(1)}, f32[128,128]{1,0:T(8,128)S(1)}, u32[]{:S(2)}, u32[]{:S(2)}) collective-permute-start(f32[128,128]{1,0:T(8,128)S(1)} %constant_dynamic-slice_fusion), channel_id=1, source_target_pairs={{0,0},{1,1},{2,2},{3,3},{4,32},{5,33},{6,34},{7,35},{8,64},{9,65},... | collective-permute-start | bytes 196616 | tf_op jit(solution)/shard_map/ppermute | solution.py:400
  47.6 46.4 %all-to-all-start.2 = ((f32[32,16,128]{2,1,0:T(8,128)}), f32[32,16,128]{2,1,0:T(8,128)S(1)}, u32[]{:S(2)}, u32[]{:S(2)}) async-start(f32[32,16,128]{2,1,0:T(8,128)} %bitcast.43), calls=%async_computation.2 | async-start | bytes 524288 | tf_op jit(solution)/shard_map/all_to_all | solution.py:432
  54.9 20.4 %collective-permute-start.7 = (f32[4,64,128]{2,1,0:T(8,128)S(1)}, f32[4,64,128]{2,1,0:T(8,128)S(1)}, u32[]{:S(2)}, u32[]{:S(2)}) collective-permute-start(f32[4,64,128]{2,1,0:T(8,128)S(1)} %get-tuple-element.18), channel_id=1, source_target_pairs={{0,56},{1,57},{2,58},{3,59},{4,24},{5,25},{6,26},{7,27},{8,120},{9... | collective-permute-start | bytes 393224 | tf_op jit(solution)/shard_map/ppermute | solution.py:429
  62.1 23.4 %collective-permute-start.6 = (f32[4,64,128]{2,1,0:T(8,128)S(1)}, f32[4,64,128]{2,1,0:T(8,128)S(1)}, u32[]{:S(2)}, u32[]{:S(2)}) collective-permute-start(f32[4,64,128]{2,1,0:T(8,128)S(1)} %get-tuple-element.19), channel_id=1, source_target_pairs={{0,24},{1,25},{2,26},{3,27},{4,56},{5,57},{6,58},{7,59},{8,88},{9,... | collective-permute-start | bytes 393224 | tf_op jit(solution)/shard_map/ppermute | solution.py:429
  63.2 24.5 %collective-permute-start.5 = (f32[4,64,128]{2,1,0:T(8,128)S(1)}, f32[4,64,128]{2,1,0:T(8,128)S(1)}, u32[]{:S(2)}, u32[]{:S(2)}) collective-permute-start(f32[4,64,128]{2,1,0:T(8,128)S(1)} %get-tuple-element.20), channel_id=1, source_target_pairs={{0,48},{1,49},{2,50},{3,51},{4,16},{5,17},{6,18},{7,19},{8,112},{9... | collective-permute-start | bytes 393224 | tf_op jit(solution)/shard_map/ppermute | solution.py:429
  67.2 29.2 %collective-permute-start.4 = (f32[4,64,128]{2,1,0:T(8,128)S(1)}, f32[4,64,128]{2,1,0:T(8,128)S(1)}, u32[]{:S(2)}, u32[]{:S(2)}) collective-permute-start(f32[4,64,128]{2,1,0:T(8,128)S(1)} %get-tuple-element.21), channel_id=1, source_target_pairs={{0,16},{1,17},{2,18},{3,19},{4,48},{5,49},{6,50},{7,51},{8,80},{9,... | collective-permute-start | bytes 393224 | tf_op jit(solution)/shard_map/ppermute | solution.py:429
  68.6 27.8 %collective-permute-start.3 = (f32[4,64,128]{2,1,0:T(8,128)S(1)}, f32[4,64,128]{2,1,0:T(8,128)S(1)}, u32[]{:S(2)}, u32[]{:S(2)}) collective-permute-start(f32[4,64,128]{2,1,0:T(8,128)S(1)} %get-tuple-element.22), channel_id=1, source_target_pairs={{0,40},{1,41},{2,42},{3,43},{4,8},{5,9},{6,10},{7,11},{8,104},{9,1... | collective-permute-start | bytes 393224 | tf_op jit(solution)/shard_map/ppermute | solution.py:429
  75.3 21.2 %collective-permute-start.2 = (f32[4,64,128]{2,1,0:T(8,128)S(1)}, f32[4,64,128]{2,1,0:T(8,128)S(1)}, u32[]{:S(2)}, u32[]{:S(2)}) collective-permute-start(f32[4,64,128]{2,1,0:T(8,128)S(1)} %get-tuple-element.23), channel_id=1, source_target_pairs={{0,8},{1,9},{2,10},{3,11},{4,40},{5,41},{6,42},{7,43},{8,72},{9,73... | collective-permute-start | bytes 393224 | tf_op jit(solution)/shard_map/ppermute | solution.py:429
  85.5 15.4 %collective-permute-start.1 = (f32[4,64,128]{2,1,0:T(8,128)S(1)}, f32[4,64,128]{2,1,0:T(8,128)S(1)}, u32[]{:S(2)}, u32[]{:S(2)}) collective-permute-start(f32[4,64,128]{2,1,0:T(8,128)S(1)} %get-tuple-element.24), channel_id=1, source_target_pairs={{0,32},{1,33},{2,34},{3,35},{4,0},{5,1},{6,2},{7,3},{8,96},{9,97},... | collective-permute-start | bytes 393224 | tf_op jit(solution)/shard_map/ppermute | solution.py:429
  87.7 17.7 %collective-permute-start = (f32[4,64,128]{2,1,0:T(8,128)S(1)}, f32[4,64,128]{2,1,0:T(8,128)S(1)}, u32[]{:S(2)}, u32[]{:S(2)}) collective-permute-start(f32[4,64,128]{2,1,0:T(8,128)S(1)} %get-tuple-element.25), channel_id=1, source_target_pairs={{0,0},{1,1},{2,2},{3,3},{4,32},{5,33},{6,34},{7,35},{8,64},{9,65},... | collective-permute-start | bytes 393224 | tf_op jit(solution)/shard_map/ppermute | solution.py:429

commit v4 on v3

--- a/solution.py
+++ b/solution.py
@@ -176,35 +176,26 @@
     return jnp.where((row // 64 == lanes_of((128, 128)) // 64) & (row % 64 == 0), 1.0, 0.0).astype(BF16)
 
 
-def attention_kernel(
-    xr_ref,
-    xc_ref,
-    bias_ref,
-    wq_ref,
-    wk_ref,
-    wv_ref,
-    single_ref,
-    wg_ref,
-    msg_ref,
-    rowpad_ref,
-    colpad_ref,
-    gate_ref,
-):
+def tokens_of(ref, n):
+    x = jnp.concatenate([ref[pl.ds(q, n, stride=4), :] for q in range(3)], axis=1)
+    return norm(x), ref[pl.ds(3, n, stride=4), :][:, 0:1]
+
+
+def query_kernel(xr_ref, wq_ref, single_ref, wg_ref, query_ref, rowpad_ref, gate_ref):
     gate_ref[...] = 1.0 / (1.0 + jnp.exp(-mm3(norm(single_ref[...]), wg_ref[...])))
-
-    def tokens(ref, n):
-        x = jnp.concatenate([ref[pl.ds(q, n, stride=4), :] for q in range(3)], axis=1)
-        return norm(x), ref[pl.ds(3, n, stride=4), :][:, 0:1]
-
-    rows, row_pad = tokens(xr_ref, 128)
-    cols, col_pad = tokens(xc_ref, 32)
+    rows, row_pad = tokens_of(xr_ref, 128)
     lane = lanes_of((16, 128))
     for m in range(4):
         a = row_pad[m * 32 : m * 32 + 16]
         b = row_pad[m * 32 + 16 : m * 32 + 32]
         rowpad_ref[m * 16 : (m + 1) * 16, :] = jnp.where(lane < 64, a, b)
+    query_ref[...] = mm3(rows, wq_ref[...]) * (24.0**-0.5)
+
+
+def attention_kernel(query_ref, xc_ref, bias_ref, wk_ref, wv_ref, msg_ref, colpad_ref):
+    cols, col_pad = tokens_of(xc_ref, 32)
     colpad_ref[...] = jnp.broadcast_to(col_pad, (32, 128))
-    query = mm3(rows, wq_ref[...]) * (24.0**-0.5)
+    query = query_ref[...]
     key = mm3(cols, wk_ref[...])
     value = mm3(cols, wv_ref[...])
     of_head = lanes_of((16, 384)) // 24 == lax.broadcasted_iota(jnp.int32, (16, 384), 0)
@@ -409,12 +400,18 @@
         name="bias",
     )(mid.reshape(4096, 128), w_bias.T)
 
-    msg, rowpad, colpad, gate = pl.pallas_call(
+    query, rowpad, gate = pl.pallas_call(
+        query_kernel,
+        in_specs=[pl.BlockSpec(memory_space=pltpu.VMEM)] * 4,
+        out_shape=[struct(128, 384), struct(64, 128), struct(4, 384)],
+        name="query",
+    )(near(rows_tok), w_query, single, w_gating)
+    msg, colpad = pl.pallas_call(
         attention_kernel,
-        in_specs=[pl.BlockSpec(memory_space=pltpu.VMEM)] * 8,
-        out_shape=[struct(512, 128), struct(64, 128), struct(32, 128), struct(4, 384)],
+        in_specs=[pl.BlockSpec(memory_space=pltpu.VMEM)] * 5,
+        out_shape=[struct(512, 128), struct(32, 128)],
         name="attention",
-    )(near(rows_tok), near(cols_tok), bias, w_query, w_key, w_value, single, w_gating)
+    )(query, near(cols_tok), bias, w_key, w_value)
 
     parts = []
     for n in range(8):

time: 111 us -> 111 us (level)
  the two profiles are of different devices: /device:TPU:38 before, /device:TPU:64 now
where the time goes in v4:
time: 111 us; the launch traced here: 110 us
  starting transfers between devices  63.1 us (57%)
  Pallas kernels  33 us (30%)
  waiting for transfers between devices  13 us (12%)
    ppermute x8, starting transfers between devices, per_device(): parts.append(lax.ppermute(piece, ALL, perm))  35 us
    pallas_call x1, Pallas kernels, per_device(): pl.pallas_call(transition_kernel, grid=(4,), in_specs=[pl.BlockSpec((4, 2...  12.8 us
    ppermute x8, waiting for transfers between devices, per_device(): parts.append(lax.ppermute(piece, ALL, perm))  10.9 us
    all_to_all x1, starting transfers between devices, per_device(): rows_tok = lax.all_to_all(tok, COL, split_axis=0, concat_axis=0, tiled=True)  8.34 us
    all_to_all x1, starting transfers between devices, per_device(): lax.all_to_all(msg.reshape(32, 16, 128), COL, split_axis=0, concat_axis=0...  7.48 us
    all_to_all x1, starting transfers between devices, per_device(): lax.all_to_all(proj.reshape(32, 64, 128), PLANE, split_axis=0, concat_axi...  7.13 us
    ppermute x1, starting transfers between devices, per_device(): cols_tok = lax.ppermute(quarter, ALL, perm)  5.19 us
    pallas_call x1, Pallas kernels, per_device(): pl.pallas_call(gradient_kernel, grid_spec=pltpu.PrefetchScalarGridSpec(nu...  5.17 us
  transfers between devices with their start and end apart: 12, of which 4 were waited for; matrix products, arithmetic and copies ran while one was open for 0% of the time, Pallas kernels for 24%

profile of v4, /device:TPU:64, one launch (start us, length us, event | category | flops | bytes accessed | tf_op | source)
XLA Modules:
  0.0 110.0 jit_solution(8222102942968510170)
XLA Ops:
  0.6 1.5 %tokens.1 = f32[32,16,128]{2,1,0:T(8,128)} custom-call(f32[4,384]{1,0:T(4,128)} %single_ref.5, s32[4]{0:T(128)} %pad_ref.1), custom_call_target="tpu_custom_call" | custom-call | tf_op jit(solution)/shard_map/tokens/pallas_call | solution.py:341
  2.2 8.3 %all-to-all-start.1 = ((f32[32,16,128]{2,1,0:T(8,128)}), f32[32,16,128]{2,1,0:T(8,128)S(1)}, u32[]{:S(2)}, u32[]{:S(2)}) async-start(f32[32,16,128]{2,1,0:T(8,128)} %tokens.1), calls=%async_computation.1 | async-start | bytes 524288 | tf_op jit(solution)/shard_map/all_to_all | solution.py:347
  10.5 12.8 %transition.1 = (f32[4,2,4,4,32,128]{5,4,3,2,1,0:T(8,128)}, f32[2,4,4,4,16,128]{5,4,3,2,1,0:T(8,128)}, f32[4,4,4,32,128]{4,3,2,1,0:T(8,128)}, bf16[4,4,4,32,128]{4,3,2,1,0:T(8,128)(2,1)}) custom-call(f32[4,2,4,4,32,128]{5,4,3,2,1,0:T(8,128)} %bitcast.38, s32[32,128]{1,0:T(8,128)} %bitcast.46, f32[128,512]{1,0:T(8,128)} %wg_ref.2, f32[128,512]{1,0:T(8,128)} %wu_ref.1, ...), custom_call_target="tpu_custom_call" | custom-call | tf_op jit(solution)/shard_map/transition/pallas_call | solution.py:350
  23.3 0.0 all-to-all-done.1
  23.3 7.1 %all-to-all-start = ((f32[32,64,128]{2,1,0:T(8,128)}), f32[32,64,128]{2,1,0:T(8,128)S(1)}, u32[]{:S(2)}, u32[]{:S(2)}) async-start(f32[32,64,128]{2,1,0:T(8,128)} %bitcast.40), calls=%async_computation | async-start | bytes 2097152 | tf_op jit(solution)/shard_map/all_to_all | solution.py:382
  30.5 5.2 %collective-permute-start.8 = (f32[128,128]{1,0:T(8,128)S(1)}, f32[128,128]{1,0:T(8,128)S(1)}, u32[]{:S(2)}, u32[]{:S(2)}) collective-permute-start(f32[128,128]{1,0:T(8,128)S(1)} %constant_dynamic-slice_fusion), channel_id=1, source_target_pairs={{0,0},{1,1},{2,2},{3,3},{4,32},{5,33},{6,34},{7,35},{8,64},{9,65},... | collective-permute-start | bytes 196616 | tf_op jit(solution)/shard_map/ppermute | solution.py:391
  35.7 4.6 %bias.1.bias_ref = f32[128,512]{1,0:T(8,128)} custom-call(f32[4096,128]{1,0:T(8,128)} %bitcast.35, f32[16,128]{1,0:T(8,128)} %bitcast.47), custom_call_target="tpu_custom_call" | custom-call | tf_op jit(solution)/shard_map/bias/pallas_call | solution.py:393
  40.2 2.6 %query.1 = (f32[128,384]{1,0:T(8,128)}, f32[64,128]{1,0:T(8,128)}, f32[4,384]{1,0:T(4,128)}) custom-call(f32[512,128]{1,0:T(8,128)S(1)} %bitcast.33, f32[384,384]{1,0:T(8,128)} %wq_ref.1, f32[4,384]{1,0:T(4,128)} %single_ref.5, f32[384,384]{1,0:T(8,128)} %wg_ref.3), custom_call_target="tpu_custom_call" | custom-call | tf_op jit(solution)/shard_map/query/pallas_call | solution.py:403
  42.8 0.0 collective-permute-done.8.xc_ref
  42.8 4.0 %attention.1 = (f32[512,128]{1,0:T(8,128)}, f32[32,128]{1,0:T(8,128)}) custom-call(f32[128,384]{1,0:T(8,128)} %get-tuple-element.16.query_ref, f32[128,128]{1,0:T(8,128)S(1)} %collective-permute-done.8.xc_ref, f32[128,512]{1,0:T(8,128)} %bias.1.bias_ref, f32[384,384]{1,0:T(8,128)} %wk_ref.1, f32[384,384]{1,0:T(8,128)} %wv_ref.1), custom_call_target="tpu_custom_call" | custom-call | tf_op jit(solution)/shard_map/attention/pallas_call | solution.py:409
  46.8 2.0 %all-to-all-done = f32[32,64,128]{2,1,0:T(8,128)S(1)} async-done(((f32[32,64,128]{2,1,0:T(8,128)}), f32[32,64,128]{2,1,0:T(8,128)S(1)}, u32[]{:S(2)}, u32[]{:S(2)}) %all-to-all-start) | async-done | bytes 1048608 | tf_op jit(solution)/shard_map/all_to_all | solution.py:382
  48.8 7.5 %all-to-all-start.2 = ((f32[32,16,128]{2,1,0:T(8,128)}), f32[32,16,128]{2,1,0:T(8,128)S(1)}, u32[]{:S(2)}, u32[]{:S(2)}) async-start(f32[32,16,128]{2,1,0:T(8,128)} %bitcast.43), calls=%async_computation.2 | async-start | bytes 524288 | tf_op jit(solution)/shard_map/all_to_all | solution.py:429
  56.4 0.1 dynamic-slice_bitcast_fusion
  56.5 7.1 %collective-permute-start.7 = (f32[4,64,128]{2,1,0:T(8,128)S(1)}, f32[4,64,128]{2,1,0:T(8,128)S(1)}, u32[]{:S(2)}, u32[]{:S(2)}) collective-permute-start(f32[4,64,128]{2,1,0:T(8,128)S(1)} %get-tuple-element.20), channel_id=1, source_target_pairs={{0,56},{1,57},{2,58},{3,59},{4,24},{5,25},{6,26},{7,27},{8,120},{9... | collective-permute-start | bytes 393224 | tf_op jit(solution)/shard_map/ppermute | solution.py:426
  63.6 1.3 %collective-permute-start.6 = (f32[4,64,128]{2,1,0:T(8,128)S(1)}, f32[4,64,128]{2,1,0:T(8,128)S(1)}, u32[]{:S(2)}, u32[]{:S(2)}) collective-permute-start(f32[4,64,128]{2,1,0:T(8,128)S(1)} %get-tuple-element.21), channel_id=1, source_target_pairs={{0,24},{1,25},{2,26},{3,27},{4,56},{5,57},{6,58},{7,59},{8,88},{9,... | collective-permute-start | bytes 393224 | tf_op jit(solution)/shard_map/ppermute | solution.py:426
  64.8 2.2 %collective-permute-start.5 = (f32[4,64,128]{2,1,0:T(8,128)S(1)}, f32[4,64,128]{2,1,0:T(8,128)S(1)}, u32[]{:S(2)}, u32[]{:S(2)}) collective-permute-start(f32[4,64,128]{2,1,0:T(8,128)S(1)} %get-tuple-element.22), channel_id=1, source_target_pairs={{0,48},{1,49},{2,50},{3,51},{4,16},{5,17},{6,18},{7,19},{8,112},{9... | collective-permute-start | bytes 393224 | tf_op jit(solution)/shard_map/ppermute | solution.py:426
  67.0 2.4 %collective-permute-start.4 = (f32[4,64,128]{2,1,0:T(8,128)S(1)}, f32[4,64,128]{2,1,0:T(8,128)S(1)}, u32[]{:S(2)}, u32[]{:S(2)}) collective-permute-start(f32[4,64,128]{2,1,0:T(8,128)S(1)} %get-tuple-element.23), channel_id=1, source_target_pairs={{0,16},{1,17},{2,18},{3,19},{4,48},{5,49},{6,50},{7,51},{8,80},{9,... | collective-permute-start | bytes 393224 | tf_op jit(solution)/shard_map/ppermute | solution.py:426
  69.4 7.1 %collective-permute-start.3 = (f32[4,64,128]{2,1,0:T(8,128)S(1)}, f32[4,64,128]{2,1,0:T(8,128)S(1)}, u32[]{:S(2)}, u32[]{:S(2)}) collective-permute-start(f32[4,64,128]{2,1,0:T(8,128)S(1)} %get-tuple-element.24), channel_id=1, source_target_pairs={{0,40},{1,41},{2,42},{3,43},{4,8},{5,9},{6,10},{7,11},{8,104},{9,1... | collective-permute-start | bytes 393224 | tf_op jit(solution)/shard_map/ppermute | solution.py:426
  76.5 2.3 %collective-permute-done.7.refs_7_ = f32[4,64,128]{2,1,0:T(8,128)S(1)} collective-permute-done((f32[4,64,128]{2,1,0:T(8,128)S(1)}, f32[4,64,128]{2,1,0:T(8,128)S(1)}, u32[]{:S(2)}, u32[]{:S(2)}) %collective-permute-start.7) | collective-permute-done | bytes 131104 | tf_op jit(solution)/shard_map/ppermute | solution.py:426
  78.8 7.9 %collective-permute-start.2 = (f32[4,64,128]{2,1,0:T(8,128)S(1)}, f32[4,64,128]{2,1,0:T(8,128)S(1)}, u32[]{:S(2)}, u32[]{:S(2)}) collective-permute-start(f32[4,64,128]{2,1,0:T(8,128)S(1)} %get-tuple-element.25), channel_id=1, source_target_pairs={{0,8},{1,9},{2,10},{3,11},{4,40},{5,41},{6,42},{7,43},{8,72},{9,73... | collective-permute-start | bytes 393224 | tf_op jit(solution)/shard_map/ppermute | solution.py:426
  86.8 0.0 collective-permute-done.6.refs_6_
  86.8 0.0 collective-permute-start.1
  86.8 0.0 collective-permute-done.5.refs_5_
  86.8 7.0 %collective-permute-start = (f32[4,64,128]{2,1,0:T(8,128)S(1)}, f32[4,64,128]{2,1,0:T(8,128)S(1)}, u32[]{:S(2)}, u32[]{:S(2)}) collective-permute-start(f32[4,64,128]{2,1,0:T(8,128)S(1)} %get-tuple-element.27), channel_id=1, source_target_pairs={{0,0},{1,1},{2,2},{3,3},{4,32},{5,33},{6,34},{7,35},{8,64},{9,65},... | collective-permute-start | bytes 393224 | tf_op jit(solution)/shard_map/ppermute | solution.py:426
  93.8 0.0 all-to-all-done.2
  93.8 2.4 %merge.1 = f32[4,384]{1,0:T(4,128)} custom-call(f32[512,128]{1,0:T(8,128)S(1)} %bitcast.34, f32[4,384]{1,0:T(4,128)} %single_ref.5, f32[4,384]{1,0:T(4,128)} %get-tuple-element.19.gate_ref, f32[384,384]{1,0:T(8,128)} %wo_ref.3), custom_call_target="tpu_custom_call" | custom-call | tf_op jit(solution)/shard_map/merge/pallas_call | solution.py:431
  96.2 0.0 collective-permute-done.4.refs_4_
  96.2 0.0 collective-permute-done.3.refs_3_
  96.2 0.0 collective-permute-done.2.refs_2_
  96.2 4.5 %collective-permute-done.1.refs_1_ = f32[4,64,128]{2,1,0:T(8,128)S(1)} collective-permute-done((f32[4,64,128]{2,1,0:T(8,128)S(1)}, f32[4,64,128]{2,1,0:T(8,128)S(1)}, u32[]{:S(2)}, u32[]{:S(2)}) %collective-permute-start.1) | collective-permute-done | bytes 131104 | tf_op jit(solution)/shard_map/ppermute | solution.py:426
  100.8 4.1 %collective-permute-done.refs_0_ = f32[4,64,128]{2,1,0:T(8,128)S(1)} collective-permute-done((f32[4,64,128]{2,1,0:T(8,128)S(1)}, f32[4,64,128]{2,1,0:T(8,128)S(1)}, u32[]{:S(2)}, u32[]{:S(2)}) %collective-permute-start) | collective-permute-done | bytes 131104 | tf_op jit(solution)/shard_map/ppermute | solution.py:426
  104.8 5.2 %gradient.1 = f32[4,2,16,32,128]{4,3,2,1,0:T(8,128)} custom-call(s32[1]{0:T(128)} %bitcast.place_ref, f32[4,64,128]{2,1,0:T(8,128)S(1)} %collective-permute-done.refs_0_, f32[4,64,128]{2,1,0:T(8,128)S(1)} %collective-permute-done.1.refs_1_, f32[4,64,128]{2,1,0:T(8,128)S(1)} %collective-permute-done.2.refs_2_, ...), custom_call_target="tpu_custom_call" | custom-call | tf_op jit(solution)/shard_map/gradient/pallas_call | solution.py:440
  (1 shorter events, 0.0 us)
Async XLA Ops:
  2.2 21.1 %all-to-all-start.1 = ((f32[32,16,128]{2,1,0:T(8,128)}), f32[32,16,128]{2,1,0:T(8,128)S(1)}, u32[]{:S(2)}, u32[]{:S(2)}) async-start(f32[32,16,128]{2,1,0:T(8,128)} %tokens.1), calls=%async_computation.1 | async-start | bytes 524288 | tf_op jit(solution)/shard_map/all_to_all | solution.py:347
  23.3 25.5 %all-to-all-start = ((f32[32,64,128]{2,1,0:T(8,128)}), f32[32,64,128]{2,1,0:T(8,128)S(1)}, u32[]{:S(2)}, u32[]{:S(2)}) async-start(f32[32,64,128]{2,1,0:T(8,128)} %bitcast.40), calls=%async_computation | async-start | bytes 2097152 | tf_op jit(solution)/shard_map/all_to_all | solution.py:382
  30.5 12.3 %collective-permute-start.8 = (f32[128,128]{1,0:T(8,128)S(1)}, f32[128,128]{1,0:T(8,128)S(1)}, u32[]{:S(2)}, u32[]{:S(2)}) collective-permute-start(f32[128,128]{1,0:T(8,128)S(1)} %constant_dynamic-slice_fusion), channel_id=1, source_target_pairs={{0,0},{1,1},{2,2},{3,3},{4,32},{5,33},{6,34},{7,35},{8,64},{9,65},... | collective-permute-start | bytes 196616 | tf_op jit(solution)/shard_map/ppermute | solution.py:391
  48.8 45.0 %all-to-all-start.2 = ((f32[32,16,128]{2,1,0:T(8,128)}), f32[32,16,128]{2,1,0:T(8,128)S(1)}, u32[]{:S(2)}, u32[]{:S(2)}) async-start(f32[32,16,128]{2,1,0:T(8,128)} %bitcast.43), calls=%async_computation.2 | async-start | bytes 524288 | tf_op jit(solution)/shard_map/all_to_all | solution.py:429
  56.5 22.4 %collective-permute-start.7 = (f32[4,64,128]{2,1,0:T(8,128)S(1)}, f32[4,64,128]{2,1,0:T(8,128)S(1)}, u32[]{:S(2)}, u32[]{:S(2)}) collective-permute-start(f32[4,64,128]{2,1,0:T(8,128)S(1)} %get-tuple-element.20), channel_id=1, source_target_pairs={{0,56},{1,57},{2,58},{3,59},{4,24},{5,25},{6,26},{7,27},{8,120},{9... | collective-permute-start | bytes 393224 | tf_op jit(solution)/shard_map/ppermute | solution.py:426
  63.6 23.2 %collective-permute-start.6 = (f32[4,64,128]{2,1,0:T(8,128)S(1)}, f32[4,64,128]{2,1,0:T(8,128)S(1)}, u32[]{:S(2)}, u32[]{:S(2)}) collective-permute-start(f32[4,64,128]{2,1,0:T(8,128)S(1)} %get-tuple-element.21), channel_id=1, source_target_pairs={{0,24},{1,25},{2,26},{3,27},{4,56},{5,57},{6,58},{7,59},{8,88},{9,... | collective-permute-start | bytes 393224 | tf_op jit(solution)/shard_map/ppermute | solution.py:426
  64.8 22.0 %collective-permute-start.5 = (f32[4,64,128]{2,1,0:T(8,128)S(1)}, f32[4,64,128]{2,1,0:T(8,128)S(1)}, u32[]{:S(2)}, u32[]{:S(2)}) collective-permute-start(f32[4,64,128]{2,1,0:T(8,128)S(1)} %get-tuple-element.22), channel_id=1, source_target_pairs={{0,48},{1,49},{2,50},{3,51},{4,16},{5,17},{6,18},{7,19},{8,112},{9... | collective-permute-start | bytes 393224 | tf_op jit(solution)/shard_map/ppermute | solution.py:426
  67.0 29.2 %collective-permute-start.4 = (f32[4,64,128]{2,1,0:T(8,128)S(1)}, f32[4,64,128]{2,1,0:T(8,128)S(1)}, u32[]{:S(2)}, u32[]{:S(2)}) collective-permute-start(f32[4,64,128]{2,1,0:T(8,128)S(1)} %get-tuple-element.23), channel_id=1, source_target_pairs={{0,16},{1,17},{2,18},{3,19},{4,48},{5,49},{6,50},{7,51},{8,80},{9,... | collective-permute-start | bytes 393224 | tf_op jit(solution)/shard_map/ppermute | solution.py:426
  69.4 26.8 %collective-permute-start.3 = (f32[4,64,128]{2,1,0:T(8,128)S(1)}, f32[4,64,128]{2,1,0:T(8,128)S(1)}, u32[]{:S(2)}, u32[]{:S(2)}) collective-permute-start(f32[4,64,128]{2,1,0:T(8,128)S(1)} %get-tuple-element.24), channel_id=1, source_target_pairs={{0,40},{1,41},{2,42},{3,43},{4,8},{5,9},{6,10},{7,11},{8,104},{9,1... | collective-permute-start | bytes 393224 | tf_op jit(solution)/shard_map/ppermute | solution.py:426
  78.8 17.4 %collective-permute-start.2 = (f32[4,64,128]{2,1,0:T(8,128)S(1)}, f32[4,64,128]{2,1,0:T(8,128)S(1)}, u32[]{:S(2)}, u32[]{:S(2)}) collective-permute-start(f32[4,64,128]{2,1,0:T(8,128)S(1)} %get-tuple-element.25), channel_id=1, source_target_pairs={{0,8},{1,9},{2,10},{3,11},{4,40},{5,41},{6,42},{7,43},{8,72},{9,73... | collective-permute-start | bytes 393224 | tf_op jit(solution)/shard_map/ppermute | solution.py:426
  86.8 14.0 %collective-permute-start.1 = (f32[4,64,128]{2,1,0:T(8,128)S(1)}, f32[4,64,128]{2,1,0:T(8,128)S(1)}, u32[]{:S(2)}, u32[]{:S(2)}) collective-permute-start(f32[4,64,128]{2,1,0:T(8,128)S(1)} %get-tuple-element.26), channel_id=1, source_target_pairs={{0,32},{1,33},{2,34},{3,35},{4,0},{5,1},{6,2},{7,3},{8,96},{9,97},... | collective-permute-start | bytes 393224 | tf_op jit(solution)/shard_map/ppermute | solution.py:426
  86.8 18.0 %collective-permute-start = (f32[4,64,128]{2,1,0:T(8,128)S(1)}, f32[4,64,128]{2,1,0:T(8,128)S(1)}, u32[]{:S(2)}, u32[]{:S(2)}) collective-permute-start(f32[4,64,128]{2,1,0:T(8,128)S(1)} %get-tuple-element.27), channel_id=1, source_target_pairs={{0,0},{1,1},{2,2},{3,3},{4,32},{5,33},{6,34},{7,35},{8,64},{9,65},... | collective-permute-start | bytes 393224 | tf_op jit(solution)/shard_map/ppermute | solution.py:426
